TPU v7x, 256 devices: a whole 4x4x8 slice. The times are simulated.
256 devices in a mesh: row: 32 (over y, z), col: 8 (over x, core).
Axes of the slice: x: 4, y: 4, z: 8, core: 2. Of those that a mesh axis runs over, the one named last changes fastest.
Arguments:
- embedding: bfloat16 [8, 32, 48, 256], P('col', 'row'), may hold values from -0.3984375 to 0.3984375
- preference: float32 [12288], P('row'), may hold values from -2.5 to -0.5
Outputs:
- responsibility: float32 [12288, 12288], P('row', 'col')
- availability: float32 [12288, 12288], P('row', 'col')
All inputs are finite; a program needn't handle non-finite values.
Results may differ from a plain program's by a relative error of at most 0.0003.
Values may be sent and summed in bfloat16 or wider, within the bound.
A program may use at most 64 MiB of HBM per device.

v0:
```python
import jax
import jax.numpy as jnp
from jax import lax
from jax.sharding import PartitionSpec as P

ITERS = 2


DAMPING = 0.5


def broadcast(block, axis, source):
    block = jnp.where(lax.axis_index(axis) == source, block, jnp.zeros_like(block))
    return lax.psum(block, axis)


def similarity(row_emb, col_emb, row_start, col_start, pref_rows):
    cross = lax.dot_general(
        row_emb, col_emb, (((1,), (1,)), ((), ())), preferred_element_type=jnp.float32
    )
    row_vals = row_emb.astype(jnp.float32)
    col_vals = col_emb.astype(jnp.float32)
    row_sq = jnp.sum(row_vals * row_vals, axis=1)
    col_sq = jnp.sum(col_vals * col_vals, axis=1)
    dist = 2.0 * cross - row_sq[:, None] - col_sq[None, :]
    row_ids = row_start + jnp.arange(row_emb.shape[0], dtype=jnp.int32)
    col_ids = col_start + jnp.arange(col_emb.shape[0], dtype=jnp.int32)
    diagonal = row_ids[:, None] == col_ids[None, :]
    return (jnp.where(diagonal, pref_rows[:, None], dist), diagonal)


def top_two(summed):
    first = jnp.max(summed, axis=1)
    hits = summed == first[:, None]
    repeats = jnp.sum(hits.astype(jnp.int32), axis=1)
    others = jnp.max(jnp.where(hits, -jnp.inf, summed), axis=1)
    second = jnp.where(repeats > 1, first, others)
    return (first, second)


def local(embedding, preference):
    rows_n = lax.axis_size("row")
    cols_n = lax.axis_size("col")
    row_idx = lax.axis_index("row")
    col_idx = lax.axis_index("col")
    mol = embedding.shape[2]
    width = embedding.shape[3]
    row_count = mol * cols_n
    col_count = mol * rows_n
    column_block = lax.all_gather(embedding, "row", axis=1, tiled=True).reshape(col_count, width)
    offset = row_idx * cols_n % rows_n
    root = row_idx * cols_n // rows_n
    own_slice = lax.dynamic_slice_in_dim(column_block, offset * mol, row_count, 0)
    row_block = broadcast(own_slice, "col", root)
    row_start = row_idx * row_count
    col_start = col_idx * col_count
    sim, diagonal = similarity(row_block, column_block, row_start, col_start, preference)
    resp = jnp.zeros_like(sim)
    avail = jnp.zeros_like(sim)
    for step in range(ITERS):
        summed = avail + sim
        local_first, local_second = top_two(summed)
        firsts, seconds = (
            lax.all_gather(local_first, "col", axis=0, tiled=True),
            lax.all_gather(local_second, "col", axis=0, tiled=True),
        )
        firsts = firsts.reshape(cols_n, row_count)
        seconds = seconds.reshape(cols_n, row_count)
        first = jnp.max(firsts, axis=0)
        at_top = firsts == first[None, :]
        repeats = jnp.sum(at_top.astype(jnp.int32), axis=0)
        others = jnp.max(jnp.where(at_top, -jnp.inf, firsts), axis=0)
        second = jnp.where(repeats > 1, first, jnp.maximum(jnp.max(seconds, axis=0), others))
        fresh = sim - jnp.where(summed == first[:, None], second[:, None], first[:, None])
        resp = DAMPING * resp + (1.0 - DAMPING) * fresh
        positive = jnp.where(diagonal, resp, jnp.maximum(resp, 0.0))
        colsum = lax.psum(jnp.sum(positive, axis=0), "row")
        renew = colsum[None, :] - positive
        renew = jnp.where(diagonal, renew, jnp.minimum(renew, 0.0))
        avail = DAMPING * avail + (1.0 - DAMPING) * renew
    return (resp, avail)


def solution(mesh):
    placed = (P("col", "row", None, None), P("row"))
    return jax.shard_map(
        local,
        mesh=mesh,
        in_specs=placed,
        out_specs=(P("row", "col"), P("row", "col")),
        check_vma=False,
    )
```

profile of v0, /device:TPU:2, one launch (start us, length us, event | category | flops | bytes accessed | tf_op | source)
XLA Modules:
  0.0 335.8 jit_solution(9302854536227118023)
XLA Ops:
  7.2 0.0 copy-start.1
  7.2 0.0 all-reduce.2.cloned.1.call-start
  7.2 53.2 %all_gather.15 = bf16[1,32,48,256]{3,2,0,1:T(8,128)(2,1)S(1)} all-gather(bf16[1,1,48,256]{3,2,0,1:T(8,128)(2,1)} %bitcast.12), channel_id=1, replica_groups=mesh['row'=32,'col'=8] {'row'}, dimensions={1}, use_global_device_ids=true | all-gather | bytes 811008 | tf_op jit(solution)/shard_map/all_gather | solution.py:50
  60.5 0.7 dynamic-slice_select_fusion
  61.2 0.0 all-reduce.2.cloned.1.call-update
  61.2 0.3 multiply_reduce_fusion
  61.5 0.1 sub.47
  61.6 59.8 %all-reduce.2.cloned.1.call-done = bf16[384,256]{1,0:T(8,128)(2,1)} async-done(((bf16[384,256]{1,0:T(8,128)(2,1)}), bf16[384,256]{1,0:T(8,128)(2,1)}) %all-reduce.2.cloned.1.call-update) | async-done | bytes 196624 | tf_op jit(solution)/shard_map/psum | solution.py:14
  121.3 1.1 multiply_reduce_fusion.1
  122.4 0.0 copy-done.1
  122.4 1.7 fusion.15
  124.1 0.4 fusion.3
  124.5 0.4 fusion.2
  124.9 11.6 %all-gather = f32[8,1,384]{2,1,0:T(1,128)S(1)} all-gather(f32[1,1,384]{2,1,0:T(1,128)S(1)} %reshape.67), channel_id=1, replica_groups=mesh['row'=32,'col'=8] {'col'}, dimensions={0}, use_global_device_ids=true | all-gather | bytes 13824 | tf_op jit(solution)/shard_map/all_gather | solution.py:64
  136.6 11.8 %all-gather.1 = f32[8,1,384]{2,1,0:T(1,128)S(1)} all-gather(f32[1,1,384]{2,1,0:T(1,128)S(1)} %reshape.69), channel_id=1, replica_groups=mesh['row'=32,'col'=8] {'col'}, dimensions={0}, use_global_device_ids=true | all-gather | bytes 13824 | tf_op jit(solution)/shard_map/all_gather | solution.py:65
  148.4 0.7 fusion.9
  149.2 76.1 %psum.22 = f32[1536]{0:T(1024)S(1)} all-reduce(f32[1536]{0:T(1024)S(1)} %fusion.9), channel_id=1, replica_groups=mesh['row'=32,'col'=8] {'row'}, use_global_device_ids=true, to_apply=%region_11.12 | all-reduce | flops 1536 | bytes 12288 | tf_op jit(solution)/shard_map/psum | solution.py:77
  225.3 1.3 fusion.14
  226.6 0.0 copy-start
  226.6 0.4 fusion.4
  227.0 0.4 fusion.5
  227.4 0.6 copy-done
  228.0 10.9 %all-gather.2 = f32[8,1,384]{2,1,0:T(1,128)S(1)} all-gather(f32[1,1,384]{2,1,0:T(1,128)S(1)} %reshape.71), channel_id=1, replica_groups=mesh['row'=32,'col'=8] {'col'}, dimensions={0}, use_global_device_ids=true | all-gather | bytes 13824 | tf_op jit(solution)/shard_map/all_gather | solution.py:64
  239.0 11.5 %all-gather.3 = f32[8,1,384]{2,1,0:T(1,128)S(1)} all-gather(f32[1,1,384]{2,1,0:T(1,128)S(1)} %reshape.73), channel_id=1, replica_groups=mesh['row'=32,'col'=8] {'col'}, dimensions={0}, use_global_device_ids=true | all-gather | bytes 13824 | tf_op jit(solution)/shard_map/all_gather | solution.py:65
  250.5 3.5 %fusion.8 = (f32[1536]{0:T(1024)S(1)}, f32[384,1536]{1,0:T(8,128)}) fusion(s32[1536]{0:T(1024)S(1)} %iota_add_fusion, s32[384]{0:T(512)S(1)} %iota_add_fusion.1, f32[384,1536]{1,0:T(8,128)S(1)} %get-tuple-element.7, f32[384]{0:T(512)S(1)} %maximum_select_fusion, f32[384,1536]{1,0:T(8,128)} %copy-done, f32[384]{0:T(512)S(1)} %reduce_max.96, ...), kind=kLoop, calls=%fused_computation.21 | loop fusion | flops 7666176 | bytes 7097856 | tf_op jit(solution)/shard_map/reduce_sum | solution.py:77
  254.0 70.6 %psum.23 = f32[1536]{0:T(1024)S(1)} all-reduce(f32[1536]{0:T(1024)S(1)} %get-tuple-element.2), channel_id=1, replica_groups=mesh['row'=32,'col'=8] {'row'}, use_global_device_ids=true, to_apply=%region_20.21 | all-reduce | flops 1536 | bytes 12288 | tf_op jit(solution)/shard_map/psum | solution.py:77
  324.7 4.3 %fusion.7 = f32[384,1536]{1,0:T(8,128)} fusion(f32[384,1536]{1,0:T(8,128)} %get-tuple-element.3, f32[384,1536]{1,0:T(8,128)S(1)} %get-tuple-element.7, f32[1536]{0:T(1024)S(1)} %psum.23, f32[1536]{0:T(1024)S(1)} %psum.22, f32[384]{0:T(512)S(1)} %maximum_select_fusion.1, f32[384]{0:T(512)S(1)} %reduce_max.91, s32[1536]{0:T(1024)S(1)} %iota_add_fusion, ...), kind=kLoop, calls=%fused_computation.17 | loop fusion | flops 10616832 | bytes 7100928 | tf_op jit(solution)/shard_map/add | solution.py:80
  (18 shorter events, 0.2 us)
Async XLA Ops:
  7.2 115.3 %copy-start.1 = (f32[384]{0:T(512)S(1)}, f32[384]{0:T(512)}, u32[]{:S(2)}) copy-start(f32[384]{0:T(512)} %param.3) | copy-start | bytes 4612
  7.2 114.2 %all-reduce.2.cloned.1.call-start = ((), (), s32[]{:S(2)}) async-start(), calls=%async_computation | async-start | bytes 393216 | tf_op jit(solution)/shard_map/psum | solution.py:14
  226.6 1.4 copy-start
Sparse Core Ops, SparseCore 0:
  61.3 59.9 all-reduce.1
where the time goes:
time: 338 us; the launch traced here: 336 us
  blocking collectives  246 us (73%)
  waiting for transfers between devices  59.8 us (18%)
  between operations  14.2 us (4%)
  other arithmetic  13.7 us (4%)
    psum x2, blocking collectives, local(): colsum = lax.psum(jnp.sum(positive, axis=0), 'row')  147 us
    psum x1, waiting for transfers between devices, broadcast(): return lax.psum(block, axis)  59.8 us
    all_gather x1, blocking collectives, local(): lax.all_gather(embedding, 'row', axis=1, tiled=True)  53.2 us
    all_gather x2, blocking collectives, local(): lax.all_gather(local_second, 'col', axis=0, tiled=True)  23.2 us
    all_gather x2, blocking collectives, local(): lax.all_gather(local_first, 'col', axis=0, tiled=True)  22.5 us
  transfers between devices with their start and end apart: 1, of which 1 were waited for; matrix products, arithmetic and copies ran while one was open for 0% of the time, Pallas kernels for 0%

commit v1 on v0

--- a/solution.py
+++ b/solution.py
@@ -1,6 +1,10 @@
+import functools
+
 import jax
 import jax.numpy as jnp
 from jax import lax
+from jax.experimental import pallas as pl
+from jax.experimental.pallas import tpu as pltpu
 from jax.sharding import PartitionSpec as P
 
 ITERS = 2
@@ -8,10 +12,127 @@
 
 DAMPING = 0.5
 
-
-def broadcast(block, axis, source):
-    block = jnp.where(lax.axis_index(axis) == source, block, jnp.zeros_like(block))
-    return lax.psum(block, axis)
+MESH = pl.DeviceIdType.MESH
+VMEM = pl.BlockSpec(memory_space=pltpu.VMEM)
+
+
+def params(cid):
+    return pltpu.CompilerParams(collective_id=cid, has_side_effects=True)
+
+
+def embed_kernel(n_row, n_col, chunk_ref, colb_ref, rowb_ref, send_c, send_r, recv_c, recv_r):
+    r = lax.axis_index("row")
+    c = lax.axis_index("col")
+    g = c * n_row + r
+    target_row = g // n_col
+    my_slot = g % n_col
+    peers = [(lax.rem(r + d, n_row), c) for d in range(1, n_row)]
+    targets = [(target_row, j) for j in range(n_col)]
+    sources = []
+    for s in range(n_col):
+        gs = r * n_col + s
+        sources.append((gs % n_row, gs // n_row))
+
+    def differs(dev):
+        return jnp.logical_or(dev[0] != r, dev[1] != c)
+
+    barrier = pltpu.get_barrier_semaphore()
+    for dev in peers:
+        pl.semaphore_signal(barrier, inc=1, device_id=dev, device_id_type=MESH)
+    for dev in targets + sources:
+        @pl.when(differs(dev))
+        def _():
+            pl.semaphore_signal(barrier, inc=1, device_id=dev, device_id_type=MESH)
+    self_in = (target_row == r).astype(jnp.int32)
+    pl.semaphore_wait(barrier, (n_row - 1) + 2 * (n_col - self_in))
+
+    local_c = pltpu.make_async_copy(chunk_ref, colb_ref.at[r], recv_c.at[r])
+    local_c.start()
+    copies = []
+    for i, dev in enumerate(peers):
+        cp = pltpu.make_async_remote_copy(
+            src_ref=chunk_ref, dst_ref=colb_ref.at[r], send_sem=send_c.at[i],
+            recv_sem=recv_c.at[r], device_id=dev, device_id_type=MESH)
+        cp.start()
+        copies.append(cp)
+    row_copies = []
+    for j, dev in enumerate(targets):
+        cp = pltpu.make_async_remote_copy(
+            src_ref=chunk_ref, dst_ref=rowb_ref.at[my_slot], send_sem=send_r.at[j],
+            recv_sem=recv_r.at[my_slot], device_id=dev, device_id_type=MESH)
+        row_copies.append(cp)
+
+        @pl.when(differs(dev))
+        def _():
+            cp.start()
+
+        @pl.when(jnp.logical_not(differs(dev)))
+        def _():
+            pltpu.make_async_copy(chunk_ref, rowb_ref.at[my_slot], recv_r.at[my_slot]).start()
+
+    for cp in copies:
+        cp.wait_send()
+    for j, dev in enumerate(targets):
+        @pl.when(differs(dev))
+        def _():
+            row_copies[j].wait_send()
+    for s in range(n_row):
+        pltpu.make_async_copy(chunk_ref, colb_ref.at[s], recv_c.at[s]).wait()
+    for s in range(n_col):
+        pltpu.make_async_copy(chunk_ref, rowb_ref.at[s], recv_r.at[s]).wait()
+
+
+def distribute(chunk, n_row, n_col):
+    mol, width = chunk.shape
+    return pl.pallas_call(
+        functools.partial(embed_kernel, n_row, n_col),
+        out_shape=(jax.ShapeDtypeStruct((n_row, mol, width), chunk.dtype),
+                   jax.ShapeDtypeStruct((n_col, mol, width), chunk.dtype)),
+        in_specs=[VMEM],
+        out_specs=(VMEM, VMEM),
+        scratch_shapes=[
+            pltpu.SemaphoreType.DMA((n_row - 1,)),
+            pltpu.SemaphoreType.DMA((n_col,)),
+            pltpu.SemaphoreType.DMA((n_row,)),
+            pltpu.SemaphoreType.DMA((n_col,)),
+        ],
+        compiler_params=params(0),
+    )(chunk)
+
+
+def gather_kernel(axis, n, src_ref, out_ref, send_sem, recv_sem):
+    me = lax.axis_index(axis)
+    peers = [lax.rem(me + d, n) for d in range(1, n)]
+    barrier = pltpu.get_barrier_semaphore()
+    for p in peers:
+        pl.semaphore_signal(barrier, inc=1, device_id={axis: p}, device_id_type=MESH)
+    pl.semaphore_wait(barrier, n - 1)
+    pltpu.make_async_copy(src_ref, out_ref.at[me], recv_sem.at[me]).start()
+    copies = []
+    for i, p in enumerate(peers):
+        cp = pltpu.make_async_remote_copy(
+            src_ref=src_ref, dst_ref=out_ref.at[me], send_sem=send_sem.at[i],
+            recv_sem=recv_sem.at[me], device_id={axis: p}, device_id_type=MESH)
+        cp.start()
+        copies.append(cp)
+    for cp in copies:
+        cp.wait_send()
+    for s in range(n):
+        pltpu.make_async_copy(src_ref, out_ref.at[s], recv_sem.at[s]).wait()
+
+
+def gather(x, axis, n, cid):
+    return pl.pallas_call(
+        functools.partial(gather_kernel, axis, n),
+        out_shape=jax.ShapeDtypeStruct((n,) + x.shape, x.dtype),
+        in_specs=[VMEM],
+        out_specs=VMEM,
+        scratch_shapes=[
+            pltpu.SemaphoreType.DMA((n - 1,)),
+            pltpu.SemaphoreType.DMA((n,)),
+        ],
+        compiler_params=params(cid),
+    )(x)
 
 
 def similarity(row_emb, col_emb, row_start, col_start, pref_rows):
@@ -47,11 +168,9 @@
     width = embedding.shape[3]
     row_count = mol * cols_n
     col_count = mol * rows_n
-    column_block = lax.all_gather(embedding, "row", axis=1, tiled=True).reshape(col_count, width)
-    offset = row_idx * cols_n % rows_n
-    root = row_idx * cols_n // rows_n
-    own_slice = lax.dynamic_slice_in_dim(column_block, offset * mol, row_count, 0)
-    row_block = broadcast(own_slice, "col", root)
+    colb, rowb = distribute(embedding.reshape(mol, width), rows_n, cols_n)
+    column_block = colb.reshape(col_count, width)
+    row_block = rowb.reshape(row_count, width)
     row_start = row_idx * row_count
     col_start = col_idx * col_count
     sim, diagonal = similarity(row_block, column_block, row_start, col_start, preference)
@@ -60,12 +179,9 @@
     for step in range(ITERS):
         summed = avail + sim
         local_first, local_second = top_two(summed)
-        firsts, seconds = (
-            lax.all_gather(local_first, "col", axis=0, tiled=True),
-            lax.all_gather(local_second, "col", axis=0, tiled=True),
-        )
-        firsts = firsts.reshape(cols_n, row_count)
-        seconds = seconds.reshape(cols_n, row_count)
+        both = gather(jnp.stack([local_first, local_second]), "col", cols_n, 1 + 2 * step)
+        firsts = both[:, 0, :]
+        seconds = both[:, 1, :]
         first = jnp.max(firsts, axis=0)
         at_top = firsts == first[None, :]
         repeats = jnp.sum(at_top.astype(jnp.int32), axis=0)
@@ -74,7 +190,8 @@
         fresh = sim - jnp.where(summed == first[:, None], second[:, None], first[:, None])
         resp = DAMPING * resp + (1.0 - DAMPING) * fresh
         positive = jnp.where(diagonal, resp, jnp.maximum(resp, 0.0))
-        colsum = lax.psum(jnp.sum(positive, axis=0), "row")
+        partial = jnp.sum(positive, axis=0)
+        colsum = jnp.sum(gather(partial[None, :], "row", rows_n, 2 + 2 * step), axis=(0, 1))
         renew = colsum[None, :] - positive
         renew = jnp.where(diagonal, renew, jnp.minimum(renew, 0.0))
         avail = DAMPING * avail + (1.0 - DAMPING) * renew

time: 338 us -> 109 us (0.32)
  blocking collectives: 246 us -> 0 us
  Pallas kernels: 0 us -> 83.1 us
  waiting for transfers between devices: 59.8 us -> 0 us
  between operations: 14.2 us -> 0.76 us
  other arithmetic: 13.7 us -> 18.9 us
    psum x2 -> x0, blocking collectives: 147 us -> none  [local(): colsum = lax.psum(jnp.sum(positive, axis=0), 'row')]
    all_gather x5 -> x0, blocking collectives: 99 us -> none  [the longest x1 53.2 us: local(): lax.all_gather(embedding, 'row', axis=1, tiled=True)]
    pallas_call x0 -> x5, Pallas kernels: none -> 83.1 us  [the longest x4 45 us: gather(): pl.pallas_call(functools.partial(gather_kernel, axis, n), out_shape=jax.S...]
    psum x1 -> x0, waiting for transfers between devices: 59.8 us -> none  [broadcast(): return lax.psum(block, axis)]
  transfers between devices with their start and end apart: 1 -> 0, of which waited for: 1 -> 0; matrix products, arithmetic and copies ran while one was open for 0% -> 0% of each run, Pallas kernels for 0% -> 0%
where the time goes in v1:
time: 109 us; the launch traced here: 107 us
  Pallas kernels  83.1 us (76%)
  other arithmetic  18.9 us (17%)
  local copies, waits for them, and re-layouts  1.95 us (2%)
  matrix products  1.95 us (2%)
    pallas_call x4, Pallas kernels, gather(): pl.pallas_call(functools.partial(gather_kernel, axis, n), out_shape=jax.S...  45 us
    pallas_call x1, Pallas kernels, distribute(): pl.pallas_call(functools.partial(embed_kernel, n_row, n_col), out_shape=(...  38 us
    add x1, other arithmetic, local(): avail = DAMPING * avail + (1.0 - DAMPING) * renew  4.3 us
    reduce_sum x2, other arithmetic, local(): partial = jnp.sum(positive, axis=0)  4.21 us

profile of v1, /device:TPU:2, one launch (start us, length us, event | category | flops | bytes accessed | tf_op | source)
XLA Modules:
  0.0 106.6 jit_solution(12345699661240848398)
XLA Ops:
  0.7 38.0 %shard_map.41 = (bf16[32,48,256]{2,1,0:T(8,128)(2,1)}, bf16[8,48,256]{2,1,0:T(8,128)(2,1)}) custom-call(bf16[48,256]{1,0:T(8,128)(2,1)} %bitcast.16), custom_call_target="tpu_custom_call" | custom-call | tf_op jit(solution)/shard_map/pallas_call | solution.py:87
  38.7 1.0 multiply_reduce_fusion.1
  39.8 0.1 sub.42
  39.8 1.4 %multiply_reduce_fusion = f32[32,48]{1,0:T(8,128)S(1)} fusion(bf16[32,48,256]{2,1,0:T(8,128)(2,1)} %get-tuple-element.5), kind=kLoop, calls=%fused_computation.23 | loop fusion | flops 1178112 | bytes 792576 | tf_op jit(solution)/shard_map/reduce_sum | solution.py:145
  41.3 0.1 sub.45
  41.3 1.9 %fusion.15 = (f32[384]{0:T(512)S(1)}, f32[384,1536]{1,0:T(8,128)S(1)}) fusion(f32[1536]{0:T(1024)S(1)} %sub.45, f32[384]{0:T(512)S(1)} %sub.42, bf16[384,256]{1,0:T(8,128)(2,1)} %bitcast.15, bf16[1536,256]{1,0:T(8,128)(2,1)} %bitcast.14, f32[384]{0:T(512)} %param.3, s32[1536]{0:T(1024)S(1)} %iota_add_fusion, s32[384]{0:T(512)S(1)} %iota_add_fusion.1), kind=kOutput, calls=%fused_computation.49 | convolution fusion | flops 305528448 | bytes 3360768 | tf_op jit(solution)/shard_map/dot_general | solution.py:139
  43.3 0.4 fusion.3
  43.7 0.4 fusion.2
  44.1 0.6 pad_maximum_fusion.src_ref
  44.7 7.5 %shard_map.42 = f32[8,2,384]{2,1,0:T(2,128)} custom-call(f32[2,384]{1,0:T(2,128)} %pad_maximum_fusion.src_ref), custom_call_target="tpu_custom_call" | custom-call | tf_op jit(solution)/shard_map/pallas_call | solution.py:125
  52.2 0.9 slice_reduce_fusion.1
  53.1 0.7 fusion.9
  53.8 0.6 broadcast_in_dim.67.src_ref
  54.4 16.0 %shard_map.43 = f32[32,1,1536]{2,1,0:T(1,128)} custom-call(f32[1,1536]{1,0:T(1,128)} %broadcast_in_dim.67.src_ref), custom_call_target="tpu_custom_call" | custom-call | tf_op jit(solution)/shard_map/pallas_call | solution.py:125
  70.4 1.1 reduce_sum.95
  71.5 1.2 %fusion.14 = (f32[384]{0:T(512)S(1)}, f32[384,1536]{1,0:T(8,128)S(1)}) fusion(f32[384,1536]{1,0:T(8,128)S(1)} %get-tuple-element.17, f32[384]{0:T(512)S(1)} %maximum_select_fusion.1, f32[384]{0:T(512)S(1)} %get-tuple-element.9, f32[1536]{0:T(1024)S(1)} %reduce_sum.95, s32[1536]{0:T(1024)S(1)} %iota_add_fusion, s32[384]{0:T(512)S(1)} %iota_add_fusion.1), kind=kLoop, calls=%fused_computation.48 | loop fusion | flops 7667328 | bytes 4737024 | tf_op jit(solution)/shard_map/reduce_max | solution.py:154
  72.7 0.0 copy-start
  72.7 0.4 fusion.5
  73.1 0.4 fusion.4
  73.5 0.6 copy-done
  74.1 0.6 pad_maximum_fusion.1.src_ref
  74.7 6.5 %shard_map.44 = f32[8,2,384]{2,1,0:T(2,128)} custom-call(f32[2,384]{1,0:T(2,128)} %pad_maximum_fusion.1.src_ref), custom_call_target="tpu_custom_call" | custom-call | tf_op jit(solution)/shard_map/pallas_call | solution.py:125
  81.3 0.9 slice_reduce_fusion
  82.2 3.5 %fusion.8 = (f32[1536]{0:T(1024)S(1)}, f32[384,1536]{1,0:T(8,128)}) fusion(s32[1536]{0:T(1024)S(1)} %iota_add_fusion, s32[384]{0:T(512)S(1)} %iota_add_fusion.1, f32[384,1536]{1,0:T(8,128)S(1)} %get-tuple-element.17, f32[384]{0:T(512)S(1)} %maximum_select_fusion, f32[384,1536]{1,0:T(8,128)} %copy-done, f32[384]{0:T(512)S(1)} %get-tuple-element.7, ...), kind=kLoop, calls=%fused_computation.21 | loop fusion | flops 7666176 | bytes 7097856 | tf_op jit(solution)/shard_map/reduce_sum | solution.py:193
  85.7 0.6 broadcast_in_dim.69.src_ref
  86.3 15.0 %shard_map.45 = f32[32,1,1536]{2,1,0:T(1,128)} custom-call(f32[1,1536]{1,0:T(1,128)} %broadcast_in_dim.69.src_ref), custom_call_target="tpu_custom_call" | custom-call | tf_op jit(solution)/shard_map/pallas_call | solution.py:125
  101.3 1.1 reduce_sum.99
  102.3 4.3 %fusion.7 = f32[384,1536]{1,0:T(8,128)} fusion(f32[384,1536]{1,0:T(8,128)} %get-tuple-element.11, f32[384,1536]{1,0:T(8,128)S(1)} %get-tuple-element.17, f32[1536]{0:T(1024)S(1)} %reduce_sum.99, f32[1536]{0:T(1024)S(1)} %reduce_sum.95, f32[384]{0:T(512)S(1)} %maximum_select_fusion.1, f32[384]{0:T(512)S(1)} %get-tuple-element.9, s32[1536]{0:T(1024)S(1)} %iota_add_fusion, ...), kind=kLoop, calls=%fused_computation.17 | loop fusion | flops 10616832 | bytes 7100928 | tf_op jit(solution)/shard_map/add | solution.py:197
  (14 shorter events, 0.1 us)
Async XLA Ops:
  72.7 1.4 %copy-start = (f32[384,1536]{1,0:T(8,128)}, f32[384,1536]{1,0:T(8,128)S(1)}, u32[]{:S(2)}) copy-start(f32[384,1536]{1,0:T(8,128)S(1)} %get-tuple-element.13) | copy-start | bytes 7077892

commit v2 on v1

--- a/solution.py
+++ b/solution.py
@@ -12,6 +12,8 @@
 
 DAMPING = 0.5
 
+INNER = 8
+
 MESH = pl.DeviceIdType.MESH
 VMEM = pl.BlockSpec(memory_space=pltpu.VMEM)
 
@@ -20,13 +22,17 @@
     return pltpu.CompilerParams(collective_id=cid, has_side_effects=True)
 
 
-def embed_kernel(n_row, n_col, chunk_ref, colb_ref, rowb_ref, send_c, send_r, recv_c, recv_r):
+def embed_kernel(n_row, n_col, inner, chunk_ref, colb_ref, rowb_ref, send_z, send_y, send_r, recv_c, recv_b, recv_r):
     r = lax.axis_index("row")
     c = lax.axis_index("col")
+    outer = n_row // inner
+    y = r // inner
+    z = r % inner
     g = c * n_row + r
     target_row = g // n_col
     my_slot = g % n_col
-    peers = [(lax.rem(r + d, n_row), c) for d in range(1, n_row)]
+    zpeers = [(y * inner + lax.rem(z + d, inner), c) for d in range(1, inner)]
+    ypeers = [(lax.rem(y + d, outer) * inner + z, c) for d in range(1, outer)]
     targets = [(target_row, j) for j in range(n_col)]
     sources = []
     for s in range(n_col):
@@ -37,24 +43,23 @@
         return jnp.logical_or(dev[0] != r, dev[1] != c)
 
     barrier = pltpu.get_barrier_semaphore()
-    for dev in peers:
+    for dev in zpeers + ypeers:
         pl.semaphore_signal(barrier, inc=1, device_id=dev, device_id_type=MESH)
     for dev in targets + sources:
         @pl.when(differs(dev))
         def _():
             pl.semaphore_signal(barrier, inc=1, device_id=dev, device_id_type=MESH)
     self_in = (target_row == r).astype(jnp.int32)
-    pl.semaphore_wait(barrier, (n_row - 1) + 2 * (n_col - self_in))
-
-    local_c = pltpu.make_async_copy(chunk_ref, colb_ref.at[r], recv_c.at[r])
-    local_c.start()
-    copies = []
-    for i, dev in enumerate(peers):
-        cp = pltpu.make_async_remote_copy(
-            src_ref=chunk_ref, dst_ref=colb_ref.at[r], send_sem=send_c.at[i],
-            recv_sem=recv_c.at[r], device_id=dev, device_id_type=MESH)
-        cp.start()
-        copies.append(cp)
+    pl.semaphore_wait(barrier, (inner - 1) + (outer - 1) + 2 * (n_col - self_in))
+
+    pltpu.make_async_copy(chunk_ref, colb_ref.at[r], recv_c.at[z]).start()
+    zcopies = []
+    for i, dev in enumerate(zpeers):
+        cp = pltpu.make_async_remote_copy(
+            src_ref=chunk_ref, dst_ref=colb_ref.at[r], send_sem=send_z.at[i],
+            recv_sem=recv_c.at[z], device_id=dev, device_id_type=MESH)
+        cp.start()
+        zcopies.append(cp)
     row_copies = []
     for j, dev in enumerate(targets):
         cp = pltpu.make_async_remote_copy(
@@ -70,34 +75,108 @@
         def _():
             pltpu.make_async_copy(chunk_ref, rowb_ref.at[my_slot], recv_r.at[my_slot]).start()
 
-    for cp in copies:
+    for s in range(inner):
+        pltpu.make_async_copy(chunk_ref, colb_ref.at[y * inner + s], recv_c.at[s]).wait()
+    block = colb_ref.at[pl.ds(y * inner, inner)]
+    ycopies = []
+    for i, dev in enumerate(ypeers):
+        cp = pltpu.make_async_remote_copy(
+            src_ref=block, dst_ref=block, send_sem=send_y.at[i],
+            recv_sem=recv_b.at[y], device_id=dev, device_id_type=MESH)
+        cp.start()
+        ycopies.append(cp)
+
+    for cp in zcopies + ycopies:
         cp.wait_send()
     for j, dev in enumerate(targets):
         @pl.when(differs(dev))
         def _():
             row_copies[j].wait_send()
-    for s in range(n_row):
-        pltpu.make_async_copy(chunk_ref, colb_ref.at[s], recv_c.at[s]).wait()
+    for d in range(1, outer):
+        yo = lax.rem(y + d, outer)
+        other = colb_ref.at[pl.ds(yo * inner, inner)]
+        pltpu.make_async_copy(other, other, recv_b.at[yo]).wait()
     for s in range(n_col):
         pltpu.make_async_copy(chunk_ref, rowb_ref.at[s], recv_r.at[s]).wait()
 
 
-def distribute(chunk, n_row, n_col):
+def distribute(chunk, n_row, n_col, inner):
     mol, width = chunk.shape
+    outer = n_row // inner
     return pl.pallas_call(
-        functools.partial(embed_kernel, n_row, n_col),
+        functools.partial(embed_kernel, n_row, n_col, inner),
         out_shape=(jax.ShapeDtypeStruct((n_row, mol, width), chunk.dtype),
                    jax.ShapeDtypeStruct((n_col, mol, width), chunk.dtype)),
         in_specs=[VMEM],
         out_specs=(VMEM, VMEM),
         scratch_shapes=[
-            pltpu.SemaphoreType.DMA((n_row - 1,)),
+            pltpu.SemaphoreType.DMA((inner - 1,)),
+            pltpu.SemaphoreType.DMA((outer - 1,)),
             pltpu.SemaphoreType.DMA((n_col,)),
-            pltpu.SemaphoreType.DMA((n_row,)),
+            pltpu.SemaphoreType.DMA((inner,)),
+            pltpu.SemaphoreType.DMA((outer,)),
             pltpu.SemaphoreType.DMA((n_col,)),
         ],
         compiler_params=params(0),
     )(chunk)
+
+
+def colsum_kernel(n, inner, part_ref, out_ref, buf1, zsum, buf2, send_z, send_y, recv_z, recv_y):
+    r = lax.axis_index("row")
+    outer = n // inner
+    y = r // inner
+    z = r % inner
+    zpeers = [y * inner + lax.rem(z + d, inner) for d in range(1, inner)]
+    ypeers = [lax.rem(y + d, outer) * inner + z for d in range(1, outer)]
+    barrier = pltpu.get_barrier_semaphore()
+    for p in zpeers + ypeers:
+        pl.semaphore_signal(barrier, inc=1, device_id={"row": p}, device_id_type=MESH)
+    pl.semaphore_wait(barrier, (inner - 1) + (outer - 1))
+    pltpu.make_async_copy(part_ref, buf1.at[pl.ds(z, 1)], recv_z.at[z]).start()
+    zcopies = []
+    for i, p in enumerate(zpeers):
+        cp = pltpu.make_async_remote_copy(
+            src_ref=part_ref, dst_ref=buf1.at[pl.ds(z, 1)], send_sem=send_z.at[i],
+            recv_sem=recv_z.at[z], device_id={"row": p}, device_id_type=MESH)
+        cp.start()
+        zcopies.append(cp)
+    for s in range(inner):
+        pltpu.make_async_copy(part_ref, buf1.at[pl.ds(s, 1)], recv_z.at[s]).wait()
+    zsum[...] = jnp.sum(buf1[...], axis=0, keepdims=True)
+    pltpu.make_async_copy(zsum, buf2.at[pl.ds(y, 1)], recv_y.at[y]).start()
+    ycopies = []
+    for i, p in enumerate(ypeers):
+        cp = pltpu.make_async_remote_copy(
+            src_ref=zsum, dst_ref=buf2.at[pl.ds(y, 1)], send_sem=send_y.at[i],
+            recv_sem=recv_y.at[y], device_id={"row": p}, device_id_type=MESH)
+        cp.start()
+        ycopies.append(cp)
+    for cp in zcopies + ycopies:
+        cp.wait_send()
+    for s in range(outer):
+        pltpu.make_async_copy(zsum, buf2.at[pl.ds(s, 1)], recv_y.at[s]).wait()
+    out_ref[...] = jnp.sum(buf2[...], axis=0, keepdims=True)
+
+
+def row_sum(part, n, inner, cid):
+    outer = n // inner
+    width = part.shape[1]
+    return pl.pallas_call(
+        functools.partial(colsum_kernel, n, inner),
+        out_shape=jax.ShapeDtypeStruct((1, width), part.dtype),
+        in_specs=[VMEM],
+        out_specs=VMEM,
+        scratch_shapes=[
+            pltpu.VMEM((inner, width), part.dtype),
+            pltpu.VMEM((1, width), part.dtype),
+            pltpu.VMEM((outer, width), part.dtype),
+            pltpu.SemaphoreType.DMA((inner - 1,)),
+            pltpu.SemaphoreType.DMA((outer - 1,)),
+            pltpu.SemaphoreType.DMA((inner,)),
+            pltpu.SemaphoreType.DMA((outer,)),
+        ],
+        compiler_params=params(cid),
+    )(part)
 
 
 def gather_kernel(axis, n, src_ref, out_ref, send_sem, recv_sem):
@@ -168,7 +247,7 @@
     width = embedding.shape[3]
     row_count = mol * cols_n
     col_count = mol * rows_n
-    colb, rowb = distribute(embedding.reshape(mol, width), rows_n, cols_n)
+    colb, rowb = distribute(embedding.reshape(mol, width), rows_n, cols_n, INNER)
     column_block = colb.reshape(col_count, width)
     row_block = rowb.reshape(row_count, width)
     row_start = row_idx * row_count
@@ -191,7 +270,7 @@
         resp = DAMPING * resp + (1.0 - DAMPING) * fresh
         positive = jnp.where(diagonal, resp, jnp.maximum(resp, 0.0))
         partial = jnp.sum(positive, axis=0)
-        colsum = jnp.sum(gather(partial[None, :], "row", rows_n, 2 + 2 * step), axis=(0, 1))
+        colsum = row_sum(partial[None, :], rows_n, INNER, 2 + 2 * step)[0]
         renew = colsum[None, :] - positive
         renew = jnp.where(diagonal, renew, jnp.minimum(renew, 0.0))
         avail = DAMPING * avail + (1.0 - DAMPING) * renew

time: 109 us -> 99 us (0.908); the launches traced: 107 us -> 98.2 us
  Pallas kernels: 83.1 us -> 75.2 us
    pallas_call x4 -> x2, Pallas kernels: 45 us -> 14 us  [gather(): pl.pallas_call(functools.partial(gather_kernel, axis, n), out_shape=jax.S...]
    pallas_call x1 -> x3, Pallas kernels: 38 us -> 61.2 us  [the longest x1 32.3 us: distribute(): pl.pallas_call(functools.partial(embed_kernel, n_row, n_col, inner), out_...]
    reduce_sum x2 -> x0, other arithmetic: 2.12 us -> none  [local(): jnp.sum(gather(partial[None, :], 'row', rows_n, 2 + 2 * step), axis=(0, 1))]
    pallas_call x0 -> x2, other arithmetic: none -> 1.43 us  [row_sum(): pl.pallas_call(functools.partial(colsum_kernel, n, inner), out_shape=jax....]
where the time goes in v2:
time: 99 us; the launch traced here: 98.2 us
  Pallas kernels  75.2 us (76%)
  other arithmetic  18.4 us (19%)
  local copies, waits for them, and re-layouts  1.97 us (2%)
  matrix products  1.95 us (2%)
    pallas_call x1, Pallas kernels, distribute(): pl.pallas_call(functools.partial(embed_kernel, n_row, n_col, inner), out_...  32.3 us
    pallas_call x2, Pallas kernels, row_sum(): pl.pallas_call(functools.partial(colsum_kernel, n, inner), out_shape=jax....  28.8 us
    pallas_call x2, Pallas kernels, gather(): pl.pallas_call(functools.partial(gather_kernel, axis, n), out_shape=jax.S...  14 us
    add x1, other arithmetic, local(): avail = DAMPING * avail + (1.0 - DAMPING) * renew  4.34 us
    reduce_sum x2, other arithmetic, local(): partial = jnp.sum(positive, axis=0)  4.25 us

profile of v2, /device:TPU:2, one launch (start us, length us, event | category | flops | bytes accessed | tf_op | source)
XLA Modules:
  0.0 98.2 jit_solution(7525751248210517154)
XLA Ops:
  0.7 32.3 %shard_map.41 = (bf16[32,48,256]{2,1,0:T(8,128)(2,1)}, bf16[8,48,256]{2,1,0:T(8,128)(2,1)}) custom-call(bf16[48,256]{1,0:T(8,128)(2,1)} %bitcast.16), custom_call_target="tpu_custom_call" | custom-call | tf_op jit(solution)/shard_map/pallas_call | solution.py:106
  33.0 1.0 %multiply_reduce_fusion.1 = f32[8,48]{1,0:T(8,128)S(1)} fusion(bf16[8,48,256]{2,1,0:T(8,128)(2,1)} %get-tuple-element.4), kind=kLoop, calls=%fused_computation.24 | loop fusion | flops 294528 | bytes 198144 | tf_op jit(solution)/shard_map/reduce_sum | solution.py:223
  34.1 0.1 sub.46
  34.1 1.4 %multiply_reduce_fusion = f32[32,48]{1,0:T(8,128)S(1)} fusion(bf16[32,48,256]{2,1,0:T(8,128)(2,1)} %get-tuple-element.5), kind=kLoop, calls=%fused_computation.23 | loop fusion | flops 1178112 | bytes 792576 | tf_op jit(solution)/shard_map/reduce_sum | solution.py:224
  35.6 0.1 sub.49
  35.6 2.0 %fusion.15 = (f32[384]{0:T(512)S(1)}, f32[384,1536]{1,0:T(8,128)S(1)}) fusion(f32[1536]{0:T(1024)S(1)} %sub.49, f32[384]{0:T(512)S(1)} %sub.46, bf16[384,256]{1,0:T(8,128)(2,1)} %bitcast.15, bf16[1536,256]{1,0:T(8,128)(2,1)} %bitcast.14, f32[384]{0:T(512)} %param.3, s32[1536]{0:T(1024)S(1)} %iota_add_fusion, s32[384]{0:T(512)S(1)} %iota_add_fusion.1), kind=kOutput, calls=%fused_computation.49 | convolution fusion | flops 305528448 | bytes 3360768 | tf_op jit(solution)/shard_map/dot_general | solution.py:218
  37.6 0.4 fusion.3
  38.0 0.4 fusion.2
  38.4 0.6 pad_maximum_fusion.src_ref
  39.0 7.4 %shard_map.42 = f32[8,2,384]{2,1,0:T(2,128)} custom-call(f32[2,384]{1,0:T(2,128)} %pad_maximum_fusion.src_ref), custom_call_target="tpu_custom_call" | custom-call | tf_op jit(solution)/shard_map/pallas_call | solution.py:204
  46.4 0.9 slice_reduce_fusion.1
  47.4 0.7 fusion.9
  48.1 0.6 broadcast_in_dim.65.part_ref
  48.7 14.8 %shard_map.43 = f32[1,1536]{1,0:T(1,128)} custom-call(f32[1,1536]{1,0:T(1,128)} %broadcast_in_dim.65.part_ref), custom_call_target="tpu_custom_call" | custom-call | tf_op jit(solution)/shard_map/pallas_call | solution.py:164
  63.5 0.7 reduce.6
  64.2 1.3 %fusion.14 = (f32[384]{0:T(512)S(1)}, f32[384,1536]{1,0:T(8,128)S(1)}) fusion(f32[384,1536]{1,0:T(8,128)S(1)} %get-tuple-element.17, f32[384]{0:T(512)S(1)} %maximum_select_fusion.1, f32[384]{0:T(512)S(1)} %get-tuple-element.9, f32[1536]{0:T(1024)S(1)} %reduce.6, s32[1536]{0:T(1024)S(1)} %iota_add_fusion, s32[384]{0:T(512)S(1)} %iota_add_fusion.1), kind=kLoop, calls=%fused_computation.48 | loop fusion | flops 7667328 | bytes 4737024 | tf_op jit(solution)/shard_map/reduce_max | solution.py:233
  65.5 0.0 copy-start
  65.5 0.4 fusion.5
  65.9 0.4 fusion.4
  66.3 0.6 copy-done
  66.9 0.6 pad_maximum_fusion.1.src_ref
  67.5 6.6 %shard_map.44 = f32[8,2,384]{2,1,0:T(2,128)} custom-call(f32[2,384]{1,0:T(2,128)} %pad_maximum_fusion.1.src_ref), custom_call_target="tpu_custom_call" | custom-call | tf_op jit(solution)/shard_map/pallas_call | solution.py:204
  74.1 0.9 slice_reduce_fusion
  75.0 3.5 %fusion.8 = (f32[1536]{0:T(1024)S(1)}, f32[384,1536]{1,0:T(8,128)}) fusion(s32[1536]{0:T(1024)S(1)} %iota_add_fusion, s32[384]{0:T(512)S(1)} %iota_add_fusion.1, f32[384,1536]{1,0:T(8,128)S(1)} %get-tuple-element.17, f32[384]{0:T(512)S(1)} %maximum_select_fusion, f32[384,1536]{1,0:T(8,128)} %copy-done, f32[384]{0:T(512)S(1)} %get-tuple-element.7, ...), kind=kLoop, calls=%fused_computation.21 | loop fusion | flops 7666176 | bytes 7097856 | tf_op jit(solution)/shard_map/reduce_sum | solution.py:272
  78.5 0.6 broadcast_in_dim.67.part_ref
  79.1 14.1 %shard_map.45 = f32[1,1536]{1,0:T(1,128)} custom-call(f32[1,1536]{1,0:T(1,128)} %broadcast_in_dim.67.part_ref), custom_call_target="tpu_custom_call" | custom-call | tf_op jit(solution)/shard_map/pallas_call | solution.py:164
  93.2 0.7 reduce.7
  93.9 4.3 %fusion.7 = f32[384,1536]{1,0:T(8,128)} fusion(f32[384,1536]{1,0:T(8,128)} %get-tuple-element.11, f32[384,1536]{1,0:T(8,128)S(1)} %get-tuple-element.17, f32[1536]{0:T(1024)S(1)} %reduce.7, f32[1536]{0:T(1024)S(1)} %reduce.6, f32[384]{0:T(512)S(1)} %maximum_select_fusion.1, f32[384]{0:T(512)S(1)} %get-tuple-element.9, s32[1536]{0:T(1024)S(1)} %iota_add_fusion, ...), kind=kLoop, calls=%fused_computation.17 | loop fusion | flops 10616832 | bytes 7100928 | tf_op jit(solution)/shard_map/add | solution.py:276
  (14 shorter events, 0.1 us)
Async XLA Ops:
  65.5 1.4 %copy-start = (f32[384,1536]{1,0:T(8,128)}, f32[384,1536]{1,0:T(8,128)S(1)}, u32[]{:S(2)}) copy-start(f32[384,1536]{1,0:T(8,128)S(1)} %get-tuple-element.13) | copy-start | bytes 7077892

commit v3 on v2

--- a/solution.py
+++ b/solution.py
@@ -214,6 +214,174 @@
     )(x)
 
 
+def iteration_kernel(n_row, n_col, inner, chunk, first_step, *refs):
+    if first_step:
+        (sim_ref, resp_out, avail_out, fcol, scol, pack, buf_f, buf_s, zpart, buf1, zsum, buf2,
+         send_t, recv_t, send_z, send_y, recv_z, recv_y) = refs
+        avail_ref = resp_ref = None
+    else:
+        (sim_ref, avail_ref, resp_ref, resp_out, avail_out, fcol, scol, pack, buf_f, buf_s, zpart,
+         buf1, zsum, buf2, send_t, recv_t, send_z, send_y, recv_z, recv_y) = refs
+    rows, cols = sim_ref.shape
+    r = lax.axis_index("row")
+    c = lax.axis_index("col")
+    outer = n_row // inner
+    y = r // inner
+    z = r % inner
+    cpeers = [lax.rem(c + d, n_col) for d in range(1, n_col)]
+    zpeers = [y * inner + lax.rem(z + d, inner) for d in range(1, inner)]
+    ypeers = [lax.rem(y + d, outer) * inner + z for d in range(1, outer)]
+    barrier = pltpu.get_barrier_semaphore()
+    for p in cpeers:
+        pl.semaphore_signal(barrier, inc=1, device_id={"col": p}, device_id_type=MESH)
+    for p in zpeers + ypeers:
+        pl.semaphore_signal(barrier, inc=1, device_id={"row": p}, device_id_type=MESH)
+    pl.semaphore_wait(barrier, (n_col - 1) + (inner - 1) + (outer - 1))
+
+    row_start = r * rows
+    col_start = c * cols
+    n_chunks = rows // chunk
+
+    def summed_at(i0):
+        s = sim_ref[pl.ds(i0, chunk), :]
+        if first_step:
+            return s, s
+        return s, avail_ref[pl.ds(i0, chunk), :] + s
+
+    def top_body(i, carry):
+        i0 = pl.multiple_of(i * chunk, chunk)
+        s, summed = summed_at(i0)
+        first = jnp.max(summed, axis=1, keepdims=True)
+        hits = summed == first
+        repeats = jnp.sum(hits.astype(jnp.float32), axis=1, keepdims=True)
+        others = jnp.max(jnp.where(hits, -jnp.inf, summed), axis=1, keepdims=True)
+        second = jnp.where(repeats > 1.0, first, others)
+        fcol[pl.ds(i0, chunk), :] = jnp.broadcast_to(first, (chunk, 128))
+        scol[pl.ds(i0, chunk), :] = jnp.broadcast_to(second, (chunk, 128))
+        return carry
+
+    lax.fori_loop(0, n_chunks, top_body, 0)
+    pack[0:1, :] = fcol[...].T[0:1, :]
+    pack[1:2, :] = scol[...].T[0:1, :]
+
+    tcopies = []
+    for k, (src, dst) in enumerate(((pack.at[0:1], buf_f), (pack.at[1:2], buf_s))):
+        pltpu.make_async_copy(src, dst.at[pl.ds(c, 1)], recv_t.at[k, c]).start()
+        for i, p in enumerate(cpeers):
+            cp = pltpu.make_async_remote_copy(
+                src_ref=src, dst_ref=dst.at[pl.ds(c, 1)], send_sem=send_t.at[k, i],
+                recv_sem=recv_t.at[k, c], device_id={"col": p}, device_id_type=MESH)
+            cp.start()
+            tcopies.append(cp)
+    for k, dst in enumerate((buf_f, buf_s)):
+        for s in range(n_col):
+            pltpu.make_async_copy(pack.at[0:1], dst.at[pl.ds(s, 1)], recv_t.at[k, s]).wait()
+    firsts = buf_f[...]
+    seconds = buf_s[...]
+    first = jnp.max(firsts, axis=0, keepdims=True)
+    at_top = firsts == first
+    repeats = jnp.sum(at_top.astype(jnp.float32), axis=0, keepdims=True)
+    others = jnp.max(jnp.where(at_top, -jnp.inf, firsts), axis=0, keepdims=True)
+    second = jnp.where(repeats > 1.0, first, jnp.maximum(jnp.max(seconds, axis=0, keepdims=True), others))
+    fcol[...] = jnp.broadcast_to(first, (128, rows)).T
+    scol[...] = jnp.broadcast_to(second, (128, rows)).T
+
+    col_ids = col_start + lax.broadcasted_iota(jnp.int32, (chunk, cols), 1)
+
+    def diag_at(i0):
+        row_ids = row_start + i0 + lax.broadcasted_iota(jnp.int32, (chunk, cols), 0)
+        return row_ids == col_ids
+
+    def resp_body(i, acc):
+        i0 = pl.multiple_of(i * chunk, chunk)
+        s, summed = summed_at(i0)
+        f = fcol[pl.ds(i0, chunk), 0:1]
+        sc = scol[pl.ds(i0, chunk), 0:1]
+        fresh = s - jnp.where(summed == f, sc, f)
+        if first_step:
+            resp = (1.0 - DAMPING) * fresh
+        else:
+            resp = DAMPING * resp_ref[pl.ds(i0, chunk), :] + (1.0 - DAMPING) * fresh
+        resp_out[pl.ds(i0, chunk), :] = resp
+        positive = jnp.where(diag_at(i0), resp, jnp.maximum(resp, 0.0))
+        return acc + jnp.sum(positive, axis=0, keepdims=True)
+
+    zpart[...] = lax.fori_loop(0, n_chunks, resp_body, jnp.zeros((1, cols), jnp.float32))
+
+    pltpu.make_async_copy(zpart, buf1.at[pl.ds(z, 1)], recv_z.at[z]).start()
+    zcopies = []
+    for i, p in enumerate(zpeers):
+        cp = pltpu.make_async_remote_copy(
+            src_ref=zpart, dst_ref=buf1.at[pl.ds(z, 1)], send_sem=send_z.at[i],
+            recv_sem=recv_z.at[z], device_id={"row": p}, device_id_type=MESH)
+        cp.start()
+        zcopies.append(cp)
+    for s in range(inner):
+        pltpu.make_async_copy(zpart, buf1.at[pl.ds(s, 1)], recv_z.at[s]).wait()
+    zsum[...] = jnp.sum(buf1[...], axis=0, keepdims=True)
+    pltpu.make_async_copy(zsum, buf2.at[pl.ds(y, 1)], recv_y.at[y]).start()
+    ycopies = []
+    for i, p in enumerate(ypeers):
+        cp = pltpu.make_async_remote_copy(
+            src_ref=zsum, dst_ref=buf2.at[pl.ds(y, 1)], send_sem=send_y.at[i],
+            recv_sem=recv_y.at[y], device_id={"row": p}, device_id_type=MESH)
+        cp.start()
+        ycopies.append(cp)
+    for s in range(outer):
+        pltpu.make_async_copy(zsum, buf2.at[pl.ds(s, 1)], recv_y.at[s]).wait()
+    colsum = jnp.sum(buf2[...], axis=0, keepdims=True)
+
+    def avail_body(i, carry):
+        i0 = pl.multiple_of(i * chunk, chunk)
+        resp = resp_out[pl.ds(i0, chunk), :]
+        diag = diag_at(i0)
+        positive = jnp.where(diag, resp, jnp.maximum(resp, 0.0))
+        renew = colsum - positive
+        renew = jnp.where(diag, renew, jnp.minimum(renew, 0.0))
+        if first_step:
+            avail_out[pl.ds(i0, chunk), :] = (1.0 - DAMPING) * renew
+        else:
+            avail_out[pl.ds(i0, chunk), :] = DAMPING * avail_ref[pl.ds(i0, chunk), :] + (1.0 - DAMPING) * renew
+        return carry
+
+    lax.fori_loop(0, n_chunks, avail_body, 0)
+    for cp in tcopies + zcopies + ycopies:
+        cp.wait_send()
+
+
+def iterate(sim, avail, resp, n_row, n_col, inner, cid):
+    rows, cols = sim.shape
+    outer = n_row // inner
+    first_step = avail is None
+    operands = (sim,) if first_step else (sim, avail, resp)
+    f32 = jnp.float32
+    return pl.pallas_call(
+        functools.partial(iteration_kernel, n_row, n_col, inner, 32, first_step),
+        out_shape=(jax.ShapeDtypeStruct((rows, cols), f32), jax.ShapeDtypeStruct((rows, cols), f32)),
+        in_specs=[VMEM] * len(operands),
+        out_specs=(VMEM, VMEM),
+        scratch_shapes=[
+            pltpu.VMEM((rows, 128), f32),
+            pltpu.VMEM((rows, 128), f32),
+            pltpu.VMEM((2, rows), f32),
+            pltpu.VMEM((n_col, rows), f32),
+            pltpu.VMEM((n_col, rows), f32),
+            pltpu.VMEM((1, cols), f32),
+            pltpu.VMEM((inner, cols), f32),
+            pltpu.VMEM((1, cols), f32),
+            pltpu.VMEM((outer, cols), f32),
+            pltpu.SemaphoreType.DMA((2, n_col - 1)),
+            pltpu.SemaphoreType.DMA((2, n_col)),
+            pltpu.SemaphoreType.DMA((inner - 1,)),
+            pltpu.SemaphoreType.DMA((outer - 1,)),
+            pltpu.SemaphoreType.DMA((inner,)),
+            pltpu.SemaphoreType.DMA((outer,)),
+        ],
+        compiler_params=pltpu.CompilerParams(
+            collective_id=cid, has_side_effects=True, vmem_limit_bytes=60 * 1024 * 1024),
+    )(*operands)
+
+
 def similarity(row_emb, col_emb, row_start, col_start, pref_rows):
     cross = lax.dot_general(
         row_emb, col_emb, (((1,), (1,)), ((), ())), preferred_element_type=jnp.float32
@@ -252,28 +420,10 @@
     row_block = rowb.reshape(row_count, width)
     row_start = row_idx * row_count
     col_start = col_idx * col_count
-    sim, diagonal = similarity(row_block, column_block, row_start, col_start, preference)
-    resp = jnp.zeros_like(sim)
-    avail = jnp.zeros_like(sim)
+    sim, unused = similarity(row_block, column_block, row_start, col_start, preference)
+    avail = resp = None
     for step in range(ITERS):
-        summed = avail + sim
-        local_first, local_second = top_two(summed)
-        both = gather(jnp.stack([local_first, local_second]), "col", cols_n, 1 + 2 * step)
-        firsts = both[:, 0, :]
-        seconds = both[:, 1, :]
-        first = jnp.max(firsts, axis=0)
-        at_top = firsts == first[None, :]
-        repeats = jnp.sum(at_top.astype(jnp.int32), axis=0)
-        others = jnp.max(jnp.where(at_top, -jnp.inf, firsts), axis=0)
-        second = jnp.where(repeats > 1, first, jnp.maximum(jnp.max(seconds, axis=0), others))
-        fresh = sim - jnp.where(summed == first[:, None], second[:, None], first[:, None])
-        resp = DAMPING * resp + (1.0 - DAMPING) * fresh
-        positive = jnp.where(diagonal, resp, jnp.maximum(resp, 0.0))
-        partial = jnp.sum(positive, axis=0)
-        colsum = row_sum(partial[None, :], rows_n, INNER, 2 + 2 * step)[0]
-        renew = colsum[None, :] - positive
-        renew = jnp.where(diagonal, renew, jnp.minimum(renew, 0.0))
-        avail = DAMPING * avail + (1.0 - DAMPING) * renew
+        resp, avail = iterate(sim, avail, resp, rows_n, cols_n, INNER, 1 + step)
     return (resp, avail)
 
 

time: 99 us -> 98 us (0.990)
  other arithmetic: 18.4 us -> 2.48 us
  Pallas kernels: 75.2 us -> 86.3 us
  local copies, waits for them, and re-layouts: 1.97 us -> 4.94 us
  matrix products: 1.95 us -> 3.17 us
    pallas_call x4 -> x2, Pallas kernels: 42.8 us -> 53.9 us  [iterate(): pl.pallas_call(functools.partial(iteration_kernel, n_row, n_col, inner, 3...]
    reduce_sum x6 -> x0, other arithmetic: 5.12 us -> none  [the longest x2 4.25 us: local(): partial = jnp.sum(positive, axis=0)]
    add x1 -> x0, other arithmetic: 4.34 us -> none  [local(): avail = DAMPING * avail + (1.0 - DAMPING) * renew]
    unnamed x2 -> x4, local copies, waits for them, and re-layouts: 0.61 us -> 4.78 us
    reduce_max x7 -> x0, other arithmetic: 3.77 us -> none  [the longest x2 1.71 us: local(): jnp.max(seconds, axis=0)]
    pallas_call x2 -> x0, other arithmetic: 1.43 us -> none  [row_sum(): pl.pallas_call(functools.partial(colsum_kernel, n, inner), out_shape=jax....]
    dot_general x1, matrix products: 1.95 us -> 3.17 us  [similarity(): lax.dot_general(row_emb, col_emb, (((1,), (1,)), ((), ())), preferred_ele...]
    broadcast_in_dim x2 -> x0, local copies, waits for them, and re-layouts: 1.2 us -> none  [local(): colsum = row_sum(partial[None, :], rows_n, INNER, 2 + 2 * step)[0]]
where the time goes in v3:
time: 98 us; the launch traced here: 97.6 us
  Pallas kernels  86.3 us (88%)
  local copies, waits for them, and re-layouts  4.94 us (5%)
  matrix products  3.17 us (3%)
  other arithmetic  2.48 us (3%)
    pallas_call x2, Pallas kernels, iterate(): pl.pallas_call(functools.partial(iteration_kernel, n_row, n_col, inner, 3...  53.9 us
    pallas_call x1, Pallas kernels, distribute(): pl.pallas_call(functools.partial(embed_kernel, n_row, n_col, inner), out_...  32.3 us
    unnamed x4, local copies, waits for them, and re-layouts  4.78 us
    dot_general x1, matrix products, similarity(): lax.dot_general(row_emb, col_emb, (((1,), (1,)), ((), ())), preferred_ele...  3.17 us

profile of v3, /device:TPU:2, one launch (start us, length us, event | category | flops | bytes accessed | tf_op | source)
XLA Modules:
  0.0 97.6 jit_solution(12053396249803411648)
XLA Ops:
  0.7 32.3 %shard_map.41 = (bf16[32,48,256]{2,1,0:T(8,128)(2,1)}, bf16[8,48,256]{2,1,0:T(8,128)(2,1)}) custom-call(bf16[48,256]{1,0:T(8,128)(2,1)} %bitcast.7), custom_call_target="tpu_custom_call" | custom-call | tf_op jit(solution)/shard_map/pallas_call | solution.py:106
  33.0 1.0 %multiply_reduce_fusion.1 = f32[8,48]{1,0:T(8,128)S(1)} fusion(bf16[8,48,256]{2,1,0:T(8,128)(2,1)} %get-tuple-element.6), kind=kLoop, calls=%fused_computation.5 | loop fusion | flops 294528 | bytes 198144 | tf_op jit(solution)/shard_map/reduce_sum | solution.py:391
  34.1 0.1 sub.20
  34.1 1.4 %multiply_reduce_fusion = f32[32,48]{1,0:T(8,128)S(1)} fusion(bf16[32,48,256]{2,1,0:T(8,128)(2,1)} %get-tuple-element.7), kind=kLoop, calls=%fused_computation.4 | loop fusion | flops 1178112 | bytes 792576 | tf_op jit(solution)/shard_map/reduce_sum | solution.py:392
  35.6 0.1 sub.23
  35.6 3.2 %fusion.2.refs_0_ = f32[384,1536]{1,0:T(8,128)} fusion(bf16[384,256]{1,0:T(8,128)(2,1)} %bitcast.6, bf16[1536,256]{1,0:T(8,128)(2,1)} %bitcast.5, f32[1536]{0:T(1024)S(1)} %sub.23, f32[384]{0:T(512)S(1)} %sub.20, f32[384]{0:T(512)} %param.3, s32[1536]{0:T(1024)S(1)} %iota_add_fusion, s32[384]{0:T(512)S(1)} %iota_add_fusion.1), kind=kOutput, calls=%fused_computation.3 | convolution fusion | flops 304939008 | bytes 3359232 | tf_op jit(solution)/shard_map/dot_general | solution.py:386
  38.8 27.4 %shard_map.42 = (f32[384,1536]{1,0:T(8,128)}, f32[384,1536]{1,0:T(8,128)}) custom-call(f32[384,1536]{1,0:T(8,128)} %fusion.2.refs_0_), custom_call_target="tpu_custom_call" | custom-call | tf_op jit(solution)/shard_map/pallas_call | solution.py:358
  66.2 26.6 %shard_map.43 = (f32[384,1536]{1,0:T(8,128)}, f32[384,1536]{1,0:T(8,128)}) custom-call(f32[384,1536]{1,0:T(8,128)} %fusion.2.refs_0_, f32[384,1536]{1,0:T(8,128)} %get-tuple-element.8.refs_1_, f32[384,1536]{1,0:T(8,128)} %get-tuple-element.9.refs_2_), custom_call_target="tpu_custom_call" | custom-call | tf_op jit(solution)/shard_map/pallas_call | solution.py:358
  92.8 0.0 copy-start
  92.8 3.4 %copy.6 = f32[384,1536]{1,0:T(8,128)} copy(f32[384,1536]{1,0:T(8,128)} %get-tuple-element.12) | data formatting | bytes 4718592
  96.1 0.0 copy-done
  96.2 1.4 %copy.7 = f32[384,1536]{1,0:T(8,128)} copy(f32[384,1536]{1,0:T(8,128)S(1)} %copy-done) | data formatting | bytes 4718592
  (2 shorter events, 0.0 us)
Async XLA Ops:
  92.8 3.4 %copy-start = (f32[384,1536]{1,0:T(8,128)S(1)}, f32[384,1536]{1,0:T(8,128)}, u32[]{:S(2)}) copy-start(f32[384,1536]{1,0:T(8,128)} %get-tuple-element.13) | copy-start | bytes 7077892

commit v4 on v2

--- a/solution.py
+++ b/solution.py
@@ -214,6 +214,195 @@
     )(x)
 
 
+def ap_kernel(n_row, n_col, inner, chunk, iters, rowb_ref, colb_ref, prefc_ref, resp_out, avail_out,
+              sim_s, resp_s, avail_s, fcol, scol, cq, pack, buf_f, buf_s, zpart, buf1, zsum, buf2,
+              send_t, recv_t, send_z, send_y, recv_z, recv_y):
+    rows, cols = sim_s.shape
+    r = lax.axis_index("row")
+    c = lax.axis_index("col")
+    outer = n_row // inner
+    y = r // inner
+    z = r % inner
+    cpeers = [lax.rem(c + d, n_col) for d in range(1, n_col)]
+    zpeers = [y * inner + lax.rem(z + d, inner) for d in range(1, inner)]
+    ypeers = [lax.rem(y + d, outer) * inner + z for d in range(1, outer)]
+    barrier = pltpu.get_barrier_semaphore()
+    for p in cpeers:
+        pl.semaphore_signal(barrier, inc=1, device_id={"col": p}, device_id_type=MESH)
+    for p in zpeers + ypeers:
+        pl.semaphore_signal(barrier, inc=1, device_id={"row": p}, device_id_type=MESH)
+
+    row_start = r * rows
+    col_start = c * cols
+    n_chunks = rows // chunk
+    col_ids = col_start + lax.broadcasted_iota(jnp.int32, (chunk, cols), 1)
+
+    def diag_at(i0):
+        row_ids = row_start + i0 + lax.broadcasted_iota(jnp.int32, (chunk, cols), 0)
+        return row_ids == col_ids
+
+    def record_top(i0, summed):
+        first = jnp.max(summed, axis=1, keepdims=True)
+        hits = summed == first
+        repeats = jnp.sum(hits.astype(jnp.float32), axis=1, keepdims=True)
+        others = jnp.max(jnp.where(hits, -jnp.inf, summed), axis=1, keepdims=True)
+        second = jnp.where(repeats > 1.0, first, others)
+        fcol[pl.ds(i0, chunk), :] = jnp.broadcast_to(first, (chunk, 128))
+        scol[pl.ds(i0, chunk), :] = jnp.broadcast_to(second, (chunk, 128))
+
+    cb = 128 if cols % 128 == 0 else cols
+    for j in range(cols // cb):
+        xc = colb_ref[pl.ds(j * cb, cb), :].astype(jnp.float32)
+        qc = jnp.sum(xc * xc, axis=1, keepdims=True)
+        cq[0:1, pl.ds(j * cb, cb)] = jnp.broadcast_to(qc, (cb, 128)).T[0:1, :]
+    rb = 128 if rows % 128 == 0 else rows
+    for j in range(rows // rb):
+        sim_s[pl.ds(j * rb, rb), :] = lax.dot_general(
+            rowb_ref[pl.ds(j * rb, rb), :], colb_ref[...], (((1,), (1,)), ((), ())),
+            preferred_element_type=jnp.float32)
+
+    def sim_body(i, carry):
+        i0 = pl.multiple_of(i * chunk, chunk)
+        xr = rowb_ref[pl.ds(i0, chunk), :].astype(jnp.float32)
+        rq = jnp.sum(xr * xr, axis=1, keepdims=True)
+        dist = 2.0 * sim_s[pl.ds(i0, chunk), :] - rq - cq[...]
+        s = jnp.where(diag_at(i0), prefc_ref[pl.ds(i0, chunk), :], dist)
+        sim_s[pl.ds(i0, chunk), :] = s
+        record_top(i0, s)
+        return carry
+
+    lax.fori_loop(0, n_chunks, sim_body, 0)
+    pl.semaphore_wait(barrier, (n_col - 1) + (inner - 1) + (outer - 1))
+
+    copies = []
+    for step in range(iters):
+        first_step = step == 0
+        last_step = step == iters - 1
+        resp_prev, avail_prev = resp_s, avail_s
+        resp_new, avail_new = (resp_out, avail_out) if last_step else (resp_s, avail_s)
+        pk = pack.at[step]
+        pk[0:1, :] = fcol[...].T[0:1, :]
+        pk[1:2, :] = scol[...].T[0:1, :]
+        for k, dst in enumerate((buf_f.at[step], buf_s.at[step])):
+            src = pk.at[pl.ds(k, 1)]
+            pltpu.make_async_copy(src, dst.at[pl.ds(c, 1)], recv_t.at[step, k, c]).start()
+            for i, p in enumerate(cpeers):
+                cp = pltpu.make_async_remote_copy(
+                    src_ref=src, dst_ref=dst.at[pl.ds(c, 1)], send_sem=send_t.at[step, k, i],
+                    recv_sem=recv_t.at[step, k, c], device_id={"col": p}, device_id_type=MESH)
+                cp.start()
+                copies.append(cp)
+        for k, dst in enumerate((buf_f.at[step], buf_s.at[step])):
+            for s in range(n_col):
+                pltpu.make_async_copy(pk.at[pl.ds(0, 1)], dst.at[pl.ds(s, 1)], recv_t.at[step, k, s]).wait()
+        firsts = buf_f[step]
+        seconds = buf_s[step]
+        first = jnp.max(firsts, axis=0, keepdims=True)
+        at_top = firsts == first
+        repeats = jnp.sum(at_top.astype(jnp.float32), axis=0, keepdims=True)
+        others = jnp.max(jnp.where(at_top, -jnp.inf, firsts), axis=0, keepdims=True)
+        second = jnp.where(repeats > 1.0, first, jnp.maximum(jnp.max(seconds, axis=0, keepdims=True), others))
+        fcol[...] = jnp.broadcast_to(first, (128, rows)).T
+        scol[...] = jnp.broadcast_to(second, (128, rows)).T
+
+        def resp_body(i, acc):
+            i0 = pl.multiple_of(i * chunk, chunk)
+            s = sim_s[pl.ds(i0, chunk), :]
+            summed = s if first_step else avail_prev[pl.ds(i0, chunk), :] + s
+            f = fcol[pl.ds(i0, chunk), 0:1]
+            sc = scol[pl.ds(i0, chunk), 0:1]
+            fresh = s - jnp.where(summed == f, sc, f)
+            if first_step:
+                resp = (1.0 - DAMPING) * fresh
+            else:
+                resp = DAMPING * resp_prev[pl.ds(i0, chunk), :] + (1.0 - DAMPING) * fresh
+            resp_new[pl.ds(i0, chunk), :] = resp
+            positive = jnp.where(diag_at(i0), resp, jnp.maximum(resp, 0.0))
+            return acc + jnp.sum(positive, axis=0, keepdims=True)
+
+        zp = zpart.at[step]
+        zp[...] = lax.fori_loop(0, n_chunks, resp_body, jnp.zeros((1, cols), jnp.float32))
+
+        b1 = buf1.at[step]
+        pltpu.make_async_copy(zp, b1.at[pl.ds(z, 1)], recv_z.at[step, z]).start()
+        for i, p in enumerate(zpeers):
+            cp = pltpu.make_async_remote_copy(
+                src_ref=zp, dst_ref=b1.at[pl.ds(z, 1)], send_sem=send_z.at[step, i],
+                recv_sem=recv_z.at[step, z], device_id={"row": p}, device_id_type=MESH)
+            cp.start()
+            copies.append(cp)
+        for s in range(inner):
+            pltpu.make_async_copy(zp, b1.at[pl.ds(s, 1)], recv_z.at[step, s]).wait()
+        zs = zsum.at[step]
+        zs[...] = jnp.sum(b1[...], axis=0, keepdims=True)
+        b2 = buf2.at[step]
+        pltpu.make_async_copy(zs, b2.at[pl.ds(y, 1)], recv_y.at[step, y]).start()
+        for i, p in enumerate(ypeers):
+            cp = pltpu.make_async_remote_copy(
+                src_ref=zs, dst_ref=b2.at[pl.ds(y, 1)], send_sem=send_y.at[step, i],
+                recv_sem=recv_y.at[step, y], device_id={"row": p}, device_id_type=MESH)
+            cp.start()
+            copies.append(cp)
+        for s in range(outer):
+            pltpu.make_async_copy(zs, b2.at[pl.ds(s, 1)], recv_y.at[step, s]).wait()
+        colsum = jnp.sum(b2[...], axis=0, keepdims=True)
+
+        def avail_body(i, carry):
+            i0 = pl.multiple_of(i * chunk, chunk)
+            resp = resp_new[pl.ds(i0, chunk), :]
+            diag = diag_at(i0)
+            positive = jnp.where(diag, resp, jnp.maximum(resp, 0.0))
+            renew = colsum - positive
+            renew = jnp.where(diag, renew, jnp.minimum(renew, 0.0))
+            if first_step:
+                avail = (1.0 - DAMPING) * renew
+            else:
+                avail = DAMPING * avail_prev[pl.ds(i0, chunk), :] + (1.0 - DAMPING) * renew
+            avail_new[pl.ds(i0, chunk), :] = avail
+            if not last_step:
+                record_top(i0, avail + sim_s[pl.ds(i0, chunk), :])
+            return carry
+
+        lax.fori_loop(0, n_chunks, avail_body, 0)
+    for cp in copies:
+        cp.wait_send()
+
+
+def propagate(rowb, colb, prefc, n_row, n_col, inner, iters, cid):
+    rows, cols = rowb.shape[0], colb.shape[0]
+    outer = n_row // inner
+    f32 = jnp.float32
+    return pl.pallas_call(
+        functools.partial(ap_kernel, n_row, n_col, inner, 32, iters),
+        out_shape=(jax.ShapeDtypeStruct((rows, cols), f32), jax.ShapeDtypeStruct((rows, cols), f32)),
+        in_specs=[VMEM] * 3,
+        out_specs=(VMEM, VMEM),
+        scratch_shapes=[
+            pltpu.VMEM((rows, cols), f32),
+            pltpu.VMEM((rows, cols), f32),
+            pltpu.VMEM((rows, cols), f32),
+            pltpu.VMEM((rows, 128), f32),
+            pltpu.VMEM((rows, 128), f32),
+            pltpu.VMEM((1, cols), f32),
+            pltpu.VMEM((iters, 2, rows), f32),
+            pltpu.VMEM((iters, n_col, rows), f32),
+            pltpu.VMEM((iters, n_col, rows), f32),
+            pltpu.VMEM((iters, 1, cols), f32),
+            pltpu.VMEM((iters, inner, cols), f32),
+            pltpu.VMEM((iters, 1, cols), f32),
+            pltpu.VMEM((iters, outer, cols), f32),
+            pltpu.SemaphoreType.DMA((iters, 2, n_col - 1)),
+            pltpu.SemaphoreType.DMA((iters, 2, n_col)),
+            pltpu.SemaphoreType.DMA((iters, inner - 1)),
+            pltpu.SemaphoreType.DMA((iters, outer - 1)),
+            pltpu.SemaphoreType.DMA((iters, inner)),
+            pltpu.SemaphoreType.DMA((iters, outer)),
+        ],
+        compiler_params=pltpu.CompilerParams(
+            collective_id=cid, has_side_effects=True, vmem_limit_bytes=60 * 1024 * 1024),
+    )(rowb, colb, prefc)
+
+
 def similarity(row_emb, col_emb, row_start, col_start, pref_rows):
     cross = lax.dot_general(
         row_emb, col_emb, (((1,), (1,)), ((), ())), preferred_element_type=jnp.float32
@@ -250,30 +439,7 @@
     colb, rowb = distribute(embedding.reshape(mol, width), rows_n, cols_n, INNER)
     column_block = colb.reshape(col_count, width)
     row_block = rowb.reshape(row_count, width)
-    row_start = row_idx * row_count
-    col_start = col_idx * col_count
-    sim, diagonal = similarity(row_block, column_block, row_start, col_start, preference)
-    resp = jnp.zeros_like(sim)
-    avail = jnp.zeros_like(sim)
-    for step in range(ITERS):
-        summed = avail + sim
-        local_first, local_second = top_two(summed)
-        both = gather(jnp.stack([local_first, local_second]), "col", cols_n, 1 + 2 * step)
-        firsts = both[:, 0, :]
-        seconds = both[:, 1, :]
-        first = jnp.max(firsts, axis=0)
-        at_top = firsts == first[None, :]
-        repeats = jnp.sum(at_top.astype(jnp.int32), axis=0)
-        others = jnp.max(jnp.where(at_top, -jnp.inf, firsts), axis=0)
-        second = jnp.where(repeats > 1, first, jnp.maximum(jnp.max(seconds, axis=0), others))
-        fresh = sim - jnp.where(summed == first[:, None], second[:, None], first[:, None])
-        resp = DAMPING * resp + (1.0 - DAMPING) * fresh
-        positive = jnp.where(diagonal, resp, jnp.maximum(resp, 0.0))
-        partial = jnp.sum(positive, axis=0)
-        colsum = row_sum(partial[None, :], rows_n, INNER, 2 + 2 * step)[0]
-        renew = colsum[None, :] - positive
-        renew = jnp.where(diagonal, renew, jnp.minimum(renew, 0.0))
-        avail = DAMPING * avail + (1.0 - DAMPING) * renew
+    resp, avail = propagate(row_block, column_block, preference.reshape(row_count, 1), rows_n, cols_n, INNER, ITERS, 1)
     return (resp, avail)
 
 

time: 99 us -> 83.5 us (0.84)
  other arithmetic: 18.4 us -> 0 us
  local copies, waits for them, and re-layouts: 1.97 us -> 6.26 us
  matrix products: 1.95 us -> 0 us
  Pallas kernels: 75.2 us -> 76.4 us
    reduce_sum x8 -> x0, other arithmetic: 7.59 us -> none  [the longest x2 4.25 us: local(): partial = jnp.sum(positive, axis=0)]
    add x3 -> x0, other arithmetic: 4.35 us -> none  [the longest x1 4.34 us: local(): avail = DAMPING * avail + (1.0 - DAMPING) * renew]
    unnamed x2 -> x4, local copies, waits for them, and re-layouts: 0.61 us -> 4.78 us
    reduce_max x7 -> x0, other arithmetic: 3.77 us -> none  [the longest x2 1.71 us: local(): jnp.max(seconds, axis=0)]
    dot_general x1 -> x0, matrix products: 1.95 us -> none  [similarity(): lax.dot_general(row_emb, col_emb, (((1,), (1,)), ((), ())), preferred_ele...]
    reshape x0 -> x1, local copies, waits for them, and re-layouts: none -> 1.48 us  [local(): preference.reshape(row_count, 1)]
    pallas_call x2 -> x0, other arithmetic: 1.43 us -> none  [row_sum(): pl.pallas_call(functools.partial(colsum_kernel, n, inner), out_shape=jax....]
    pallas_call x4 -> x1, Pallas kernels: 42.8 us -> 44.1 us  [propagate(): pl.pallas_call(functools.partial(ap_kernel, n_row, n_col, inner, 32, iter...]
where the time goes in v4:
time: 83.5 us; the launch traced here: 83.3 us
  Pallas kernels  76.4 us (91%)
  local copies, waits for them, and re-layouts  6.26 us (7%)
    pallas_call x1, Pallas kernels, propagate(): pl.pallas_call(functools.partial(ap_kernel, n_row, n_col, inner, 32, iter...  44.1 us
    pallas_call x1, Pallas kernels, distribute(): pl.pallas_call(functools.partial(embed_kernel, n_row, n_col, inner), out_...  32.2 us
    unnamed x4, local copies, waits for them, and re-layouts  4.78 us

profile of v4, /device:TPU:2, one launch (start us, length us, event | category | flops | bytes accessed | tf_op | source)
XLA Modules:
  0.0 83.3 jit_solution(11995328479079011112)
XLA Ops:
  0.6 1.5 %reshape.20.prefc_ref = f32[384,1]{1,0:T(8,128)} reshape(f32[384]{0:T(512)} %param.3) | data formatting | bytes 3072 | tf_op jit(solution)/shard_map/reshape | solution.py:442
  2.1 32.2 %shard_map.41 = (bf16[32,48,256]{2,1,0:T(8,128)(2,1)}, bf16[8,48,256]{2,1,0:T(8,128)(2,1)}) custom-call(bf16[48,256]{1,0:T(8,128)(2,1)} %bitcast.5), custom_call_target="tpu_custom_call" | custom-call | tf_op jit(solution)/shard_map/pallas_call | solution.py:106
  34.4 44.1 %shard_map.42 = (f32[384,1536]{1,0:T(8,128)}, f32[384,1536]{1,0:T(8,128)}) custom-call(bf16[384,256]{1,0:T(8,128)(2,1)} %bitcast.4, bf16[1536,256]{1,0:T(8,128)(2,1)} %bitcast.3, f32[384,1]{1,0:T(8,128)} %reshape.20.prefc_ref), custom_call_target="tpu_custom_call" | custom-call | tf_op jit(solution)/shard_map/pallas_call | solution.py:375
  78.5 0.0 copy-start
  78.5 3.4 %copy.7 = f32[384,1536]{1,0:T(8,128)} copy(f32[384,1536]{1,0:T(8,128)} %get-tuple-element.8) | data formatting | bytes 4718592
  81.9 0.0 copy-done
  81.9 1.4 %copy.8 = f32[384,1536]{1,0:T(8,128)} copy(f32[384,1536]{1,0:T(8,128)S(1)} %copy-done) | data formatting | bytes 4718592
Async XLA Ops:
  78.5 3.4 %copy-start = (f32[384,1536]{1,0:T(8,128)S(1)}, f32[384,1536]{1,0:T(8,128)}, u32[]{:S(2)}) copy-start(f32[384,1536]{1,0:T(8,128)} %get-tuple-element.9) | copy-start | bytes 7077892

commit v5 on v4

--- a/solution.py
+++ b/solution.py
@@ -214,8 +214,9 @@
     )(x)
 
 
-def ap_kernel(n_row, n_col, inner, chunk, iters, rowb_ref, colb_ref, prefc_ref, resp_out, avail_out,
-              sim_s, resp_s, avail_s, fcol, scol, cq, pack, buf_f, buf_s, zpart, buf1, zsum, buf2,
+def ap_kernel(n_row, n_col, inner, chunk, iters, chunk_ref, prefr_ref, resp_out, avail_out,
+              colb3, rowb3, prefc, sim_s, resp_s, avail_s, fcol, scol, cq, pack, buf_f, buf_s, zpart, buf1,
+              zsum, buf2, e_send_z, e_send_y, e_send_r, e_recv_c, e_recv_b, e_recv_r,
               send_t, recv_t, send_z, send_y, recv_z, recv_y):
     rows, cols = sim_s.shape
     r = lax.axis_index("row")
@@ -226,11 +227,78 @@
     cpeers = [lax.rem(c + d, n_col) for d in range(1, n_col)]
     zpeers = [y * inner + lax.rem(z + d, inner) for d in range(1, inner)]
     ypeers = [lax.rem(y + d, outer) * inner + z for d in range(1, outer)]
+    g = c * n_row + r
+    target_row = g // n_col
+    my_slot = g % n_col
+    targets = [(target_row, j) for j in range(n_col)]
+    sources = []
+    for s in range(n_col):
+        gs = r * n_col + s
+        sources.append((gs % n_row, gs // n_row))
+
+    def differs(dev):
+        return jnp.logical_or(dev[0] != r, dev[1] != c)
+
     barrier = pltpu.get_barrier_semaphore()
     for p in cpeers:
         pl.semaphore_signal(barrier, inc=1, device_id={"col": p}, device_id_type=MESH)
     for p in zpeers + ypeers:
         pl.semaphore_signal(barrier, inc=1, device_id={"row": p}, device_id_type=MESH)
+    for dev in targets + sources:
+        @pl.when(differs(dev))
+        def _():
+            pl.semaphore_signal(barrier, inc=1, device_id=dev, device_id_type=MESH)
+    self_in = (target_row == r).astype(jnp.int32)
+    pl.semaphore_wait(barrier, (n_col - 1) + (inner - 1) + (outer - 1) + 2 * (n_col - self_in))
+
+    copies = []
+    pltpu.make_async_copy(chunk_ref, colb3.at[r], e_recv_c.at[z]).start()
+    for i, p in enumerate(zpeers):
+        cp = pltpu.make_async_remote_copy(
+            src_ref=chunk_ref, dst_ref=colb3.at[r], send_sem=e_send_z.at[i],
+            recv_sem=e_recv_c.at[z], device_id={"row": p}, device_id_type=MESH)
+        cp.start()
+        copies.append(cp)
+    row_copies = []
+    for j, dev in enumerate(targets):
+        cp = pltpu.make_async_remote_copy(
+            src_ref=chunk_ref, dst_ref=rowb3.at[my_slot], send_sem=e_send_r.at[j],
+            recv_sem=e_recv_r.at[my_slot], device_id=dev, device_id_type=MESH)
+        row_copies.append(cp)
+
+        @pl.when(differs(dev))
+        def _():
+            cp.start()
+
+        @pl.when(jnp.logical_not(differs(dev)))
+        def _():
+            pltpu.make_async_copy(chunk_ref, rowb3.at[my_slot], e_recv_r.at[my_slot]).start()
+
+    prefc[...] = jnp.broadcast_to(prefr_ref[...], (128, rows)).T
+    for s in range(inner):
+        pltpu.make_async_copy(chunk_ref, colb3.at[y * inner + s], e_recv_c.at[s]).wait()
+    block = colb3.at[pl.ds(y * inner, inner)]
+    for i, p in enumerate(ypeers):
+        cp = pltpu.make_async_remote_copy(
+            src_ref=block, dst_ref=block, send_sem=e_send_y.at[i],
+            recv_sem=e_recv_b.at[y], device_id={"row": p}, device_id_type=MESH)
+        cp.start()
+        copies.append(cp)
+    for d in range(1, outer):
+        yo = lax.rem(y + d, outer)
+        other = colb3.at[pl.ds(yo * inner, inner)]
+        pltpu.make_async_copy(other, other, e_recv_b.at[yo]).wait()
+    for s in range(n_col):
+        pltpu.make_async_copy(chunk_ref, rowb3.at[s], e_recv_r.at[s]).wait()
+    mol = chunk_ref.shape[0]
+    colb_ref = colb3
+    rowb_ref = rowb3
+
+    def colb_rows(start, size):
+        return colb_ref[pl.ds(start // mol, size // mol)].reshape(size, -1)
+
+    def rowb_rows(start, size):
+        return rowb_ref[pl.ds(start // mol, size // mol)].reshape(size, -1)
 
     row_start = r * rows
     col_start = c * cols
@@ -250,31 +318,32 @@
         fcol[pl.ds(i0, chunk), :] = jnp.broadcast_to(first, (chunk, 128))
         scol[pl.ds(i0, chunk), :] = jnp.broadcast_to(second, (chunk, 128))
 
+    colb_all = colb_ref[...].reshape(cols, -1)
+    rowb_all = rowb_ref[...].reshape(rows, -1)
     cb = 128 if cols % 128 == 0 else cols
     for j in range(cols // cb):
-        xc = colb_ref[pl.ds(j * cb, cb), :].astype(jnp.float32)
+        xc = colb_all[j * cb:(j + 1) * cb, :].astype(jnp.float32)
         qc = jnp.sum(xc * xc, axis=1, keepdims=True)
         cq[0:1, pl.ds(j * cb, cb)] = jnp.broadcast_to(qc, (cb, 128)).T[0:1, :]
+    xr = rowb_all.astype(jnp.float32)
+    rq_s = fcol
+    rq_s[...] = jnp.broadcast_to(jnp.sum(xr * xr, axis=1, keepdims=True), (rows, 128))
     rb = 128 if rows % 128 == 0 else rows
     for j in range(rows // rb):
         sim_s[pl.ds(j * rb, rb), :] = lax.dot_general(
-            rowb_ref[pl.ds(j * rb, rb), :], colb_ref[...], (((1,), (1,)), ((), ())),
+            rowb_all[j * rb:(j + 1) * rb, :], colb_all, (((1,), (1,)), ((), ())),
             preferred_element_type=jnp.float32)
 
     def sim_body(i, carry):
         i0 = pl.multiple_of(i * chunk, chunk)
-        xr = rowb_ref[pl.ds(i0, chunk), :].astype(jnp.float32)
-        rq = jnp.sum(xr * xr, axis=1, keepdims=True)
+        rq = rq_s[pl.ds(i0, chunk), 0:1]
         dist = 2.0 * sim_s[pl.ds(i0, chunk), :] - rq - cq[...]
-        s = jnp.where(diag_at(i0), prefc_ref[pl.ds(i0, chunk), :], dist)
+        s = jnp.where(diag_at(i0), prefc[pl.ds(i0, chunk), 0:1], dist)
         sim_s[pl.ds(i0, chunk), :] = s
         record_top(i0, s)
         return carry
 
     lax.fori_loop(0, n_chunks, sim_body, 0)
-    pl.semaphore_wait(barrier, (n_col - 1) + (inner - 1) + (outer - 1))
-
-    copies = []
     for step in range(iters):
         first_step = step == 0
         last_step = step == iters - 1
@@ -366,18 +435,26 @@
         lax.fori_loop(0, n_chunks, avail_body, 0)
     for cp in copies:
         cp.wait_send()
-
-
-def propagate(rowb, colb, prefc, n_row, n_col, inner, iters, cid):
-    rows, cols = rowb.shape[0], colb.shape[0]
+    for j, dev in enumerate(targets):
+        @pl.when(differs(dev))
+        def _():
+            row_copies[j].wait_send()
+
+
+def propagate(chunk, pref_row, n_row, n_col, inner, iters, cid):
+    mol, width = chunk.shape
+    rows, cols = mol * n_col, mol * n_row
     outer = n_row // inner
     f32 = jnp.float32
     return pl.pallas_call(
         functools.partial(ap_kernel, n_row, n_col, inner, 32, iters),
         out_shape=(jax.ShapeDtypeStruct((rows, cols), f32), jax.ShapeDtypeStruct((rows, cols), f32)),
-        in_specs=[VMEM] * 3,
+        in_specs=[VMEM] * 2,
         out_specs=(VMEM, VMEM),
         scratch_shapes=[
+            pltpu.VMEM((n_row, mol, width), chunk.dtype),
+            pltpu.VMEM((n_col, mol, width), chunk.dtype),
+            pltpu.VMEM((rows, 128), f32),
             pltpu.VMEM((rows, cols), f32),
             pltpu.VMEM((rows, cols), f32),
             pltpu.VMEM((rows, cols), f32),
@@ -391,6 +468,12 @@
             pltpu.VMEM((iters, inner, cols), f32),
             pltpu.VMEM((iters, 1, cols), f32),
             pltpu.VMEM((iters, outer, cols), f32),
+            pltpu.SemaphoreType.DMA((inner - 1,)),
+            pltpu.SemaphoreType.DMA((outer - 1,)),
+            pltpu.SemaphoreType.DMA((n_col,)),
+            pltpu.SemaphoreType.DMA((inner,)),
+            pltpu.SemaphoreType.DMA((outer,)),
+            pltpu.SemaphoreType.DMA((n_col,)),
             pltpu.SemaphoreType.DMA((iters, 2, n_col - 1)),
             pltpu.SemaphoreType.DMA((iters, 2, n_col)),
             pltpu.SemaphoreType.DMA((iters, inner - 1)),
@@ -400,7 +483,7 @@
         ],
         compiler_params=pltpu.CompilerParams(
             collective_id=cid, has_side_effects=True, vmem_limit_bytes=60 * 1024 * 1024),
-    )(rowb, colb, prefc)
+    )(chunk, pref_row)
 
 
 def similarity(row_emb, col_emb, row_start, col_start, pref_rows):
@@ -436,10 +519,7 @@
     width = embedding.shape[3]
     row_count = mol * cols_n
     col_count = mol * rows_n
-    colb, rowb = distribute(embedding.reshape(mol, width), rows_n, cols_n, INNER)
-    column_block = colb.reshape(col_count, width)
-    row_block = rowb.reshape(row_count, width)
-    resp, avail = propagate(row_block, column_block, preference.reshape(row_count, 1), rows_n, cols_n, INNER, ITERS, 1)
+    resp, avail = propagate(embedding.reshape(mol, width), preference.reshape(1, row_count), rows_n, cols_n, INNER, ITERS, 0)
     return (resp, avail)
 
 

time: 83.5 us -> 80.6 us (0.965)
  Pallas kernels: 76.4 us -> 73.8 us
    pallas_call x1 -> x0, Pallas kernels: 32.2 us -> none  [distribute(): pl.pallas_call(functools.partial(embed_kernel, n_row, n_col, inner), out_...]
    pallas_call x1, Pallas kernels: 44.1 us -> 73.8 us  [propagate(): pl.pallas_call(functools.partial(ap_kernel, n_row, n_col, inner, 32, iter...]
where the time goes in v5:
time: 80.6 us; the launch traced here: 80.4 us
  Pallas kernels  73.8 us (92%)
  local copies, waits for them, and re-layouts  6.03 us (7%)
    pallas_call x1, Pallas kernels, propagate(): pl.pallas_call(functools.partial(ap_kernel, n_row, n_col, inner, 32, iter...  73.8 us
    unnamed x4, local copies, waits for them, and re-layouts  4.78 us

profile of v5, /device:TPU:2, one launch (start us, length us, event | category | flops | bytes accessed | tf_op | source)
XLA Modules:
  0.0 80.4 jit_solution(13950434934241322190)
XLA Ops:
  0.6 1.2 %reshape.11.prefr_ref = f32[1,384]{1,0:T(1,128)} reshape(f32[384]{0:T(512)} %param.3) | data formatting | bytes 3072 | tf_op jit(solution)/shard_map/reshape | solution.py:522
  1.9 73.8 %shard_map.41 = (f32[384,1536]{1,0:T(8,128)}, f32[384,1536]{1,0:T(8,128)}) custom-call(bf16[48,256]{1,0:T(8,128)(2,1)} %bitcast.1, f32[1,384]{1,0:T(1,128)} %reshape.11.prefr_ref), custom_call_target="tpu_custom_call" | custom-call | tf_op jit(solution)/shard_map/pallas_call | solution.py:449
  75.6 0.0 copy-start
  75.7 3.4 %copy.6 = f32[384,1536]{1,0:T(8,128)} copy(f32[384,1536]{1,0:T(8,128)} %get-tuple-element.4) | data formatting | bytes 4718592
  79.0 0.0 copy-done
  79.0 1.4 %copy.7 = f32[384,1536]{1,0:T(8,128)} copy(f32[384,1536]{1,0:T(8,128)S(1)} %copy-done) | data formatting | bytes 4718592
Async XLA Ops:
  75.6 3.4 %copy-start = (f32[384,1536]{1,0:T(8,128)S(1)}, f32[384,1536]{1,0:T(8,128)}, u32[]{:S(2)}) copy-start(f32[384,1536]{1,0:T(8,128)} %get-tuple-element.5) | copy-start | bytes 7077892

commit v6 on v5

--- a/solution.py
+++ b/solution.py
@@ -111,10 +111,10 @@
         out_specs=(VMEM, VMEM),
         scratch_shapes=[
             pltpu.SemaphoreType.DMA((inner - 1,)),
-            pltpu.SemaphoreType.DMA((outer - 1,)),
+            pltpu.SemaphoreType.DMA((inner, outer - 1)),
             pltpu.SemaphoreType.DMA((n_col,)),
             pltpu.SemaphoreType.DMA((inner,)),
-            pltpu.SemaphoreType.DMA((outer,)),
+            pltpu.SemaphoreType.DMA((outer, inner)),
             pltpu.SemaphoreType.DMA((n_col,)),
         ],
         compiler_params=params(0),
@@ -275,19 +275,21 @@
             pltpu.make_async_copy(chunk_ref, rowb3.at[my_slot], e_recv_r.at[my_slot]).start()
 
     prefc[...] = jnp.broadcast_to(prefr_ref[...], (128, rows)).T
-    for s in range(inner):
-        pltpu.make_async_copy(chunk_ref, colb3.at[y * inner + s], e_recv_c.at[s]).wait()
-    block = colb3.at[pl.ds(y * inner, inner)]
-    for i, p in enumerate(ypeers):
-        cp = pltpu.make_async_remote_copy(
-            src_ref=block, dst_ref=block, send_sem=e_send_y.at[i],
-            recv_sem=e_recv_b.at[y], device_id={"row": p}, device_id_type=MESH)
-        cp.start()
-        copies.append(cp)
+    for d in range(inner):
+        zs = lax.rem(z + d, inner)
+        slot = colb3.at[y * inner + zs]
+        pltpu.make_async_copy(chunk_ref, slot, e_recv_c.at[zs]).wait()
+        for i, p in enumerate(ypeers):
+            cp = pltpu.make_async_remote_copy(
+                src_ref=slot, dst_ref=slot, send_sem=e_send_y.at[d, i],
+                recv_sem=e_recv_b.at[y, zs], device_id={"row": p}, device_id_type=MESH)
+            cp.start()
+            copies.append(cp)
     for d in range(1, outer):
         yo = lax.rem(y + d, outer)
-        other = colb3.at[pl.ds(yo * inner, inner)]
-        pltpu.make_async_copy(other, other, e_recv_b.at[yo]).wait()
+        for s in range(inner):
+            other = colb3.at[yo * inner + s]
+            pltpu.make_async_copy(other, other, e_recv_b.at[yo, s]).wait()
     for s in range(n_col):
         pltpu.make_async_copy(chunk_ref, rowb3.at[s], e_recv_r.at[s]).wait()
     mol = chunk_ref.shape[0]
@@ -469,10 +471,10 @@
             pltpu.VMEM((iters, 1, cols), f32),
             pltpu.VMEM((iters, outer, cols), f32),
             pltpu.SemaphoreType.DMA((inner - 1,)),
-            pltpu.SemaphoreType.DMA((outer - 1,)),
+            pltpu.SemaphoreType.DMA((inner, outer - 1)),
             pltpu.SemaphoreType.DMA((n_col,)),
             pltpu.SemaphoreType.DMA((inner,)),
-            pltpu.SemaphoreType.DMA((outer,)),
+            pltpu.SemaphoreType.DMA((outer, inner)),
             pltpu.SemaphoreType.DMA((n_col,)),
             pltpu.SemaphoreType.DMA((iters, 2, n_col - 1)),
             pltpu.SemaphoreType.DMA((iters, 2, n_col)),

time: 80.6 us -> 79.6 us (0.988)
  Pallas kernels: 73.8 us -> 72.6 us
    pallas_call x1, Pallas kernels: 73.8 us -> 72.6 us  [propagate(): pl.pallas_call(functools.partial(ap_kernel, n_row, n_col, inner, 32, iter...]
where the time goes in v6:
time: 79.6 us; the launch traced here: 79.3 us
  Pallas kernels  72.6 us (91%)
  local copies, waits for them, and re-layouts  6.03 us (8%)
    pallas_call x1, Pallas kernels, propagate(): pl.pallas_call(functools.partial(ap_kernel, n_row, n_col, inner, 32, iter...  72.6 us
    unnamed x4, local copies, waits for them, and re-layouts  4.78 us

profile of v6, /device:TPU:2, one launch (start us, length us, event | category | flops | bytes accessed | tf_op | source)
XLA Modules:
  0.0 79.3 jit_solution(8942162503939665032)
XLA Ops:
  0.6 1.2 %reshape.11.prefr_ref = f32[1,384]{1,0:T(1,128)} reshape(f32[384]{0:T(512)} %param.3) | data formatting | bytes 3072 | tf_op jit(solution)/shard_map/reshape | solution.py:524
  1.9 72.6 %shard_map.41 = (f32[384,1536]{1,0:T(8,128)}, f32[384,1536]{1,0:T(8,128)}) custom-call(bf16[48,256]{1,0:T(8,128)(2,1)} %bitcast.1, f32[1,384]{1,0:T(1,128)} %reshape.11.prefr_ref), custom_call_target="tpu_custom_call" | custom-call | tf_op jit(solution)/shard_map/pallas_call | solution.py:451
  74.5 0.0 copy-start
  74.5 3.4 %copy.6 = f32[384,1536]{1,0:T(8,128)} copy(f32[384,1536]{1,0:T(8,128)} %get-tuple-element.4) | data formatting | bytes 4718592
  77.9 0.0 copy-done
  77.9 1.4 %copy.7 = f32[384,1536]{1,0:T(8,128)} copy(f32[384,1536]{1,0:T(8,128)S(1)} %copy-done) | data formatting | bytes 4718592
Async XLA Ops:
  74.5 3.4 %copy-start = (f32[384,1536]{1,0:T(8,128)S(1)}, f32[384,1536]{1,0:T(8,128)}, u32[]{:S(2)}) copy-start(f32[384,1536]{1,0:T(8,128)} %get-tuple-element.5) | copy-start | bytes 7077892

commit v7 on v6

--- a/solution.py
+++ b/solution.py
@@ -33,10 +33,12 @@
     my_slot = g % n_col
     zpeers = [(y * inner + lax.rem(z + d, inner), c) for d in range(1, inner)]
     ypeers = [(lax.rem(y + d, outer) * inner + z, c) for d in range(1, outer)]
-    targets = [(target_row, j) for j in range(n_col)]
+    parity = c % 2
+    sibling = c + 1 - 2 * parity
+    targets = [(target_row, 2 * x + my_slot % 2) for x in range(n_col // 2)]
     sources = []
-    for s in range(n_col):
-        gs = r * n_col + s
+    for t in range(n_col // 2):
+        gs = r * n_col + 2 * t + parity
         sources.append((gs % n_row, gs // n_row))
 
     def differs(dev):
@@ -112,7 +114,8 @@
         scratch_shapes=[
             pltpu.SemaphoreType.DMA((inner - 1,)),
             pltpu.SemaphoreType.DMA((inner, outer - 1)),
-            pltpu.SemaphoreType.DMA((n_col,)),
+            pltpu.SemaphoreType.DMA((n_col // 2,)),
+            pltpu.SemaphoreType.DMA((n_col // 2,)),
             pltpu.SemaphoreType.DMA((inner,)),
             pltpu.SemaphoreType.DMA((outer, inner)),
             pltpu.SemaphoreType.DMA((n_col,)),
@@ -216,7 +219,7 @@
 
 def ap_kernel(n_row, n_col, inner, chunk, iters, chunk_ref, prefr_ref, resp_out, avail_out,
               colb3, rowb3, prefc, sim_s, resp_s, avail_s, fcol, scol, cq, pack, buf_f, buf_s, zpart, buf1,
-              zsum, buf2, e_send_z, e_send_y, e_send_r, e_recv_c, e_recv_b, e_recv_r,
+              zsum, buf2, e_send_z, e_send_y, e_send_r, e_send_f, e_recv_c, e_recv_b, e_recv_r,
               send_t, recv_t, send_z, send_y, recv_z, recv_y):
     rows, cols = sim_s.shape
     r = lax.axis_index("row")
@@ -230,10 +233,12 @@
     g = c * n_row + r
     target_row = g // n_col
     my_slot = g % n_col
-    targets = [(target_row, j) for j in range(n_col)]
+    parity = c % 2
+    sibling = c + 1 - 2 * parity
+    targets = [(target_row, 2 * x + my_slot % 2) for x in range(n_col // 2)]
     sources = []
-    for s in range(n_col):
-        gs = r * n_col + s
+    for t in range(n_col // 2):
+        gs = r * n_col + 2 * t + parity
         sources.append((gs % n_row, gs // n_row))
 
     def differs(dev):
@@ -248,8 +253,8 @@
         @pl.when(differs(dev))
         def _():
             pl.semaphore_signal(barrier, inc=1, device_id=dev, device_id_type=MESH)
-    self_in = (target_row == r).astype(jnp.int32)
-    pl.semaphore_wait(barrier, (n_col - 1) + (inner - 1) + (outer - 1) + 2 * (n_col - self_in))
+    self_in = jnp.logical_and(target_row == r, my_slot % 2 == parity).astype(jnp.int32)
+    pl.semaphore_wait(barrier, (n_col - 1) + (inner - 1) + (outer - 1) + 2 * (n_col // 2 - self_in))
 
     copies = []
     pltpu.make_async_copy(chunk_ref, colb3.at[r], e_recv_c.at[z]).start()
@@ -290,7 +295,16 @@
         for s in range(inner):
             other = colb3.at[yo * inner + s]
             pltpu.make_async_copy(other, other, e_recv_b.at[yo, s]).wait()
-    for s in range(n_col):
+    for t in range(n_col // 2):
+        s = 2 * t + parity
+        pltpu.make_async_copy(chunk_ref, rowb3.at[s], e_recv_r.at[s]).wait()
+        cp = pltpu.make_async_remote_copy(
+            src_ref=rowb3.at[s], dst_ref=rowb3.at[s], send_sem=e_send_f.at[t],
+            recv_sem=e_recv_r.at[s], device_id={"col": sibling}, device_id_type=MESH)
+        cp.start()
+        copies.append(cp)
+    for t in range(n_col // 2):
+        s = 2 * t + 1 - parity
         pltpu.make_async_copy(chunk_ref, rowb3.at[s], e_recv_r.at[s]).wait()
     mol = chunk_ref.shape[0]
     colb_ref = colb3
@@ -472,7 +486,8 @@
             pltpu.VMEM((iters, outer, cols), f32),
             pltpu.SemaphoreType.DMA((inner - 1,)),
             pltpu.SemaphoreType.DMA((inner, outer - 1)),
-            pltpu.SemaphoreType.DMA((n_col,)),
+            pltpu.SemaphoreType.DMA((n_col // 2,)),
+            pltpu.SemaphoreType.DMA((n_col // 2,)),
             pltpu.SemaphoreType.DMA((inner,)),
             pltpu.SemaphoreType.DMA((outer, inner)),
             pltpu.SemaphoreType.DMA((n_col,)),

time: 79.6 us -> 76.4 us (0.960)
  Pallas kernels: 72.6 us -> 69.5 us
    pallas_call x1, Pallas kernels: 72.6 us -> 69.5 us  [propagate(): pl.pallas_call(functools.partial(ap_kernel, n_row, n_col, inner, 32, iter...]
where the time goes in v7:
time: 76.4 us; the launch traced here: 76.2 us
  Pallas kernels  69.5 us (91%)
  local copies, waits for them, and re-layouts  6.03 us (8%)
    pallas_call x1, Pallas kernels, propagate(): pl.pallas_call(functools.partial(ap_kernel, n_row, n_col, inner, 32, iter...  69.5 us
    unnamed x4, local copies, waits for them, and re-layouts  4.78 us

profile of v7, /device:TPU:2, one launch (start us, length us, event | category | flops | bytes accessed | tf_op | source)
XLA Modules:
  0.0 76.2 jit_solution(5708739525587983546)
XLA Ops:
  0.6 1.2 %reshape.11.prefr_ref = f32[1,384]{1,0:T(1,128)} reshape(f32[384]{0:T(512)} %param.3) | data formatting | bytes 3072 | tf_op jit(solution)/shard_map/reshape | solution.py:539
  1.9 69.5 %shard_map.41 = (f32[384,1536]{1,0:T(8,128)}, f32[384,1536]{1,0:T(8,128)}) custom-call(bf16[48,256]{1,0:T(8,128)(2,1)} %bitcast.1, f32[1,384]{1,0:T(1,128)} %reshape.11.prefr_ref), custom_call_target="tpu_custom_call" | custom-call | tf_op jit(solution)/shard_map/pallas_call | solution.py:465
  71.4 0.0 copy-start
  71.4 3.4 %copy.6 = f32[384,1536]{1,0:T(8,128)} copy(f32[384,1536]{1,0:T(8,128)} %get-tuple-element.4) | data formatting | bytes 4718592
  74.8 0.0 copy-done
  74.8 1.4 %copy.7 = f32[384,1536]{1,0:T(8,128)} copy(f32[384,1536]{1,0:T(8,128)S(1)} %copy-done) | data formatting | bytes 4718592
Async XLA Ops:
  71.4 3.4 %copy-start = (f32[384,1536]{1,0:T(8,128)S(1)}, f32[384,1536]{1,0:T(8,128)}, u32[]{:S(2)}) copy-start(f32[384,1536]{1,0:T(8,128)} %get-tuple-element.5) | copy-start | bytes 7077892

commit v8 on v7

--- a/solution.py
+++ b/solution.py
@@ -16,205 +16,6 @@
 
 MESH = pl.DeviceIdType.MESH
 VMEM = pl.BlockSpec(memory_space=pltpu.VMEM)
-
-
-def params(cid):
-    return pltpu.CompilerParams(collective_id=cid, has_side_effects=True)
-
-
-def embed_kernel(n_row, n_col, inner, chunk_ref, colb_ref, rowb_ref, send_z, send_y, send_r, recv_c, recv_b, recv_r):
-    r = lax.axis_index("row")
-    c = lax.axis_index("col")
-    outer = n_row // inner
-    y = r // inner
-    z = r % inner
-    g = c * n_row + r
-    target_row = g // n_col
-    my_slot = g % n_col
-    zpeers = [(y * inner + lax.rem(z + d, inner), c) for d in range(1, inner)]
-    ypeers = [(lax.rem(y + d, outer) * inner + z, c) for d in range(1, outer)]
-    parity = c % 2
-    sibling = c + 1 - 2 * parity
-    targets = [(target_row, 2 * x + my_slot % 2) for x in range(n_col // 2)]
-    sources = []
-    for t in range(n_col // 2):
-        gs = r * n_col + 2 * t + parity
-        sources.append((gs % n_row, gs // n_row))
-
-    def differs(dev):
-        return jnp.logical_or(dev[0] != r, dev[1] != c)
-
-    barrier = pltpu.get_barrier_semaphore()
-    for dev in zpeers + ypeers:
-        pl.semaphore_signal(barrier, inc=1, device_id=dev, device_id_type=MESH)
-    for dev in targets + sources:
-        @pl.when(differs(dev))
-        def _():
-            pl.semaphore_signal(barrier, inc=1, device_id=dev, device_id_type=MESH)
-    self_in = (target_row == r).astype(jnp.int32)
-    pl.semaphore_wait(barrier, (inner - 1) + (outer - 1) + 2 * (n_col - self_in))
-
-    pltpu.make_async_copy(chunk_ref, colb_ref.at[r], recv_c.at[z]).start()
-    zcopies = []
-    for i, dev in enumerate(zpeers):
-        cp = pltpu.make_async_remote_copy(
-            src_ref=chunk_ref, dst_ref=colb_ref.at[r], send_sem=send_z.at[i],
-            recv_sem=recv_c.at[z], device_id=dev, device_id_type=MESH)
-        cp.start()
-        zcopies.append(cp)
-    row_copies = []
-    for j, dev in enumerate(targets):
-        cp = pltpu.make_async_remote_copy(
-            src_ref=chunk_ref, dst_ref=rowb_ref.at[my_slot], send_sem=send_r.at[j],
-            recv_sem=recv_r.at[my_slot], device_id=dev, device_id_type=MESH)
-        row_copies.append(cp)
-
-        @pl.when(differs(dev))
-        def _():
-            cp.start()
-
-        @pl.when(jnp.logical_not(differs(dev)))
-        def _():
-            pltpu.make_async_copy(chunk_ref, rowb_ref.at[my_slot], recv_r.at[my_slot]).start()
-
-    for s in range(inner):
-        pltpu.make_async_copy(chunk_ref, colb_ref.at[y * inner + s], recv_c.at[s]).wait()
-    block = colb_ref.at[pl.ds(y * inner, inner)]
-    ycopies = []
-    for i, dev in enumerate(ypeers):
-        cp = pltpu.make_async_remote_copy(
-            src_ref=block, dst_ref=block, send_sem=send_y.at[i],
-            recv_sem=recv_b.at[y], device_id=dev, device_id_type=MESH)
-        cp.start()
-        ycopies.append(cp)
-
-    for cp in zcopies + ycopies:
-        cp.wait_send()
-    for j, dev in enumerate(targets):
-        @pl.when(differs(dev))
-        def _():
-            row_copies[j].wait_send()
-    for d in range(1, outer):
-        yo = lax.rem(y + d, outer)
-        other = colb_ref.at[pl.ds(yo * inner, inner)]
-        pltpu.make_async_copy(other, other, recv_b.at[yo]).wait()
-    for s in range(n_col):
-        pltpu.make_async_copy(chunk_ref, rowb_ref.at[s], recv_r.at[s]).wait()
-
-
-def distribute(chunk, n_row, n_col, inner):
-    mol, width = chunk.shape
-    outer = n_row // inner
-    return pl.pallas_call(
-        functools.partial(embed_kernel, n_row, n_col, inner),
-        out_shape=(jax.ShapeDtypeStruct((n_row, mol, width), chunk.dtype),
-                   jax.ShapeDtypeStruct((n_col, mol, width), chunk.dtype)),
-        in_specs=[VMEM],
-        out_specs=(VMEM, VMEM),
-        scratch_shapes=[
-            pltpu.SemaphoreType.DMA((inner - 1,)),
-            pltpu.SemaphoreType.DMA((inner, outer - 1)),
-            pltpu.SemaphoreType.DMA((n_col // 2,)),
-            pltpu.SemaphoreType.DMA((n_col // 2,)),
-            pltpu.SemaphoreType.DMA((inner,)),
-            pltpu.SemaphoreType.DMA((outer, inner)),
-            pltpu.SemaphoreType.DMA((n_col,)),
-        ],
-        compiler_params=params(0),
-    )(chunk)
-
-
-def colsum_kernel(n, inner, part_ref, out_ref, buf1, zsum, buf2, send_z, send_y, recv_z, recv_y):
-    r = lax.axis_index("row")
-    outer = n // inner
-    y = r // inner
-    z = r % inner
-    zpeers = [y * inner + lax.rem(z + d, inner) for d in range(1, inner)]
-    ypeers = [lax.rem(y + d, outer) * inner + z for d in range(1, outer)]
-    barrier = pltpu.get_barrier_semaphore()
-    for p in zpeers + ypeers:
-        pl.semaphore_signal(barrier, inc=1, device_id={"row": p}, device_id_type=MESH)
-    pl.semaphore_wait(barrier, (inner - 1) + (outer - 1))
-    pltpu.make_async_copy(part_ref, buf1.at[pl.ds(z, 1)], recv_z.at[z]).start()
-    zcopies = []
-    for i, p in enumerate(zpeers):
-        cp = pltpu.make_async_remote_copy(
-            src_ref=part_ref, dst_ref=buf1.at[pl.ds(z, 1)], send_sem=send_z.at[i],
-            recv_sem=recv_z.at[z], device_id={"row": p}, device_id_type=MESH)
-        cp.start()
-        zcopies.append(cp)
-    for s in range(inner):
-        pltpu.make_async_copy(part_ref, buf1.at[pl.ds(s, 1)], recv_z.at[s]).wait()
-    zsum[...] = jnp.sum(buf1[...], axis=0, keepdims=True)
-    pltpu.make_async_copy(zsum, buf2.at[pl.ds(y, 1)], recv_y.at[y]).start()
-    ycopies = []
-    for i, p in enumerate(ypeers):
-        cp = pltpu.make_async_remote_copy(
-            src_ref=zsum, dst_ref=buf2.at[pl.ds(y, 1)], send_sem=send_y.at[i],
-            recv_sem=recv_y.at[y], device_id={"row": p}, device_id_type=MESH)
-        cp.start()
-        ycopies.append(cp)
-    for cp in zcopies + ycopies:
-        cp.wait_send()
-    for s in range(outer):
-        pltpu.make_async_copy(zsum, buf2.at[pl.ds(s, 1)], recv_y.at[s]).wait()
-    out_ref[...] = jnp.sum(buf2[...], axis=0, keepdims=True)
-
-
-def row_sum(part, n, inner, cid):
-    outer = n // inner
-    width = part.shape[1]
-    return pl.pallas_call(
-        functools.partial(colsum_kernel, n, inner),
-        out_shape=jax.ShapeDtypeStruct((1, width), part.dtype),
-        in_specs=[VMEM],
-        out_specs=VMEM,
-        scratch_shapes=[
-            pltpu.VMEM((inner, width), part.dtype),
-            pltpu.VMEM((1, width), part.dtype),
-            pltpu.VMEM((outer, width), part.dtype),
-            pltpu.SemaphoreType.DMA((inner - 1,)),
-            pltpu.SemaphoreType.DMA((outer - 1,)),
-            pltpu.SemaphoreType.DMA((inner,)),
-            pltpu.SemaphoreType.DMA((outer,)),
-        ],
-        compiler_params=params(cid),
-    )(part)
-
-
-def gather_kernel(axis, n, src_ref, out_ref, send_sem, recv_sem):
-    me = lax.axis_index(axis)
-    peers = [lax.rem(me + d, n) for d in range(1, n)]
-    barrier = pltpu.get_barrier_semaphore()
-    for p in peers:
-        pl.semaphore_signal(barrier, inc=1, device_id={axis: p}, device_id_type=MESH)
-    pl.semaphore_wait(barrier, n - 1)
-    pltpu.make_async_copy(src_ref, out_ref.at[me], recv_sem.at[me]).start()
-    copies = []
-    for i, p in enumerate(peers):
-        cp = pltpu.make_async_remote_copy(
-            src_ref=src_ref, dst_ref=out_ref.at[me], send_sem=send_sem.at[i],
-            recv_sem=recv_sem.at[me], device_id={axis: p}, device_id_type=MESH)
-        cp.start()
-        copies.append(cp)
-    for cp in copies:
-        cp.wait_send()
-    for s in range(n):
-        pltpu.make_async_copy(src_ref, out_ref.at[s], recv_sem.at[s]).wait()
-
-
-def gather(x, axis, n, cid):
-    return pl.pallas_call(
-        functools.partial(gather_kernel, axis, n),
-        out_shape=jax.ShapeDtypeStruct((n,) + x.shape, x.dtype),
-        in_specs=[VMEM],
-        out_specs=VMEM,
-        scratch_shapes=[
-            pltpu.SemaphoreType.DMA((n - 1,)),
-            pltpu.SemaphoreType.DMA((n,)),
-        ],
-        compiler_params=params(cid),
-    )(x)
 
 
 def ap_kernel(n_row, n_col, inner, chunk, iters, chunk_ref, prefr_ref, resp_out, avail_out,
@@ -310,11 +111,6 @@
     colb_ref = colb3
     rowb_ref = rowb3
 
-    def colb_rows(start, size):
-        return colb_ref[pl.ds(start // mol, size // mol)].reshape(size, -1)
-
-    def rowb_rows(start, size):
-        return rowb_ref[pl.ds(start // mol, size // mol)].reshape(size, -1)
 
     row_start = r * rows
     col_start = c * cols
@@ -463,7 +259,7 @@
     outer = n_row // inner
     f32 = jnp.float32
     return pl.pallas_call(
-        functools.partial(ap_kernel, n_row, n_col, inner, 32, iters),
+        functools.partial(ap_kernel, n_row, n_col, inner, rows, iters),
         out_shape=(jax.ShapeDtypeStruct((rows, cols), f32), jax.ShapeDtypeStruct((rows, cols), f32)),
         in_specs=[VMEM] * 2,
         out_specs=(VMEM, VMEM),
@@ -503,30 +299,6 @@
     )(chunk, pref_row)
 
 
-def similarity(row_emb, col_emb, row_start, col_start, pref_rows):
-    cross = lax.dot_general(
-        row_emb, col_emb, (((1,), (1,)), ((), ())), preferred_element_type=jnp.float32
-    )
-    row_vals = row_emb.astype(jnp.float32)
-    col_vals = col_emb.astype(jnp.float32)
-    row_sq = jnp.sum(row_vals * row_vals, axis=1)
-    col_sq = jnp.sum(col_vals * col_vals, axis=1)
-    dist = 2.0 * cross - row_sq[:, None] - col_sq[None, :]
-    row_ids = row_start + jnp.arange(row_emb.shape[0], dtype=jnp.int32)
-    col_ids = col_start + jnp.arange(col_emb.shape[0], dtype=jnp.int32)
-    diagonal = row_ids[:, None] == col_ids[None, :]
-    return (jnp.where(diagonal, pref_rows[:, None], dist), diagonal)
-
-
-def top_two(summed):
-    first = jnp.max(summed, axis=1)
-    hits = summed == first[:, None]
-    repeats = jnp.sum(hits.astype(jnp.int32), axis=1)
-    others = jnp.max(jnp.where(hits, -jnp.inf, summed), axis=1)
-    second = jnp.where(repeats > 1, first, others)
-    return (first, second)
-
-
 def local(embedding, preference):
     rows_n = lax.axis_size("row")
     cols_n = lax.axis_size("col")

time: 76.4 us -> 70.3 us (0.920)
  Pallas kernels: 69.5 us -> 63.4 us
    pallas_call x1, Pallas kernels: 69.5 us -> 63.4 us  [propagate(): pl.pallas_call(functools.partial(ap_kernel, n_row, n_col, inner, rows, it...]
where the time goes in v8:
time: 70.3 us; the launch traced here: 70.1 us
  Pallas kernels  63.4 us (90%)
  local copies, waits for them, and re-layouts  6.03 us (9%)
    pallas_call x1, Pallas kernels, propagate(): pl.pallas_call(functools.partial(ap_kernel, n_row, n_col, inner, rows, it...  63.4 us
    unnamed x4, local copies, waits for them, and re-layouts  4.78 us

profile of v8, /device:TPU:2, one launch (start us, length us, event | category | flops | bytes accessed | tf_op | source)
XLA Modules:
  0.0 70.1 jit_solution(9966186117231190552)
XLA Ops:
  0.6 1.2 %reshape.11.prefr_ref = f32[1,384]{1,0:T(1,128)} reshape(f32[384]{0:T(512)} %param.3) | data formatting | bytes 3072 | tf_op jit(solution)/shard_map/reshape | solution.py:311
  1.9 63.4 %shard_map.41 = (f32[384,1536]{1,0:T(8,128)}, f32[384,1536]{1,0:T(8,128)}) custom-call(bf16[48,256]{1,0:T(8,128)(2,1)} %bitcast.1, f32[1,384]{1,0:T(1,128)} %reshape.11.prefr_ref), custom_call_target="tpu_custom_call" | custom-call | tf_op jit(solution)/shard_map/pallas_call | solution.py:261
  65.3 0.0 copy-start
  65.3 3.4 %copy.6 = f32[384,1536]{1,0:T(8,128)} copy(f32[384,1536]{1,0:T(8,128)} %get-tuple-element.4) | data formatting | bytes 4718592
  68.7 0.0 copy-done
  68.7 1.4 %copy.7 = f32[384,1536]{1,0:T(8,128)} copy(f32[384,1536]{1,0:T(8,128)S(1)} %copy-done) | data formatting | bytes 4718592
Async XLA Ops:
  65.3 3.4 %copy-start = (f32[384,1536]{1,0:T(8,128)S(1)}, f32[384,1536]{1,0:T(8,128)}, u32[]{:S(2)}) copy-start(f32[384,1536]{1,0:T(8,128)} %get-tuple-element.5) | copy-start | bytes 7077892

commit v9 on v8

--- a/solution.py
+++ b/solution.py
@@ -80,7 +80,7 @@
         def _():
             pltpu.make_async_copy(chunk_ref, rowb3.at[my_slot], e_recv_r.at[my_slot]).start()
 
-    prefc[...] = jnp.broadcast_to(prefr_ref[...], (128, rows)).T
+    prefc[...] = jnp.broadcast_to(prefr_ref[...].reshape(1, rows), (128, rows)).T
     for d in range(inner):
         zs = lax.rem(z + d, inner)
         slot = colb3.at[y * inner + zs]
@@ -308,7 +308,7 @@
     width = embedding.shape[3]
     row_count = mol * cols_n
     col_count = mol * rows_n
-    resp, avail = propagate(embedding.reshape(mol, width), preference.reshape(1, row_count), rows_n, cols_n, INNER, ITERS, 0)
+    resp, avail = propagate(embedding.reshape(mol, width), preference, rows_n, cols_n, INNER, ITERS, 0)
     return (resp, avail)
 
 

time: 70.3 us -> 69.1 us (0.983)
  local copies, waits for them, and re-layouts: 6.03 us -> 4.78 us
    reshape x1 -> x0, local copies, waits for them, and re-layouts: 1.25 us -> none  [local(): preference.reshape(1, row_count)]
where the time goes in v9:
time: 69.1 us; the launch traced here: 69 us
  Pallas kernels  63.6 us (92%)
  local copies, waits for them, and re-layouts  4.78 us (7%)
    pallas_call x1, Pallas kernels, propagate(): pl.pallas_call(functools.partial(ap_kernel, n_row, n_col, inner, rows, it...  63.6 us
    unnamed x4, local copies, waits for them, and re-layouts  4.78 us

profile of v9, /device:TPU:2, one launch (start us, length us, event | category | flops | bytes accessed | tf_op | source)
XLA Modules:
  0.0 69.0 jit_solution(18246265963711680452)
XLA Ops:
  0.6 63.6 %shard_map.41 = (f32[384,1536]{1,0:T(8,128)}, f32[384,1536]{1,0:T(8,128)}) custom-call(bf16[48,256]{1,0:T(8,128)(2,1)} %bitcast.1, f32[384]{0:T(512)} %prefr_ref.1), custom_call_target="tpu_custom_call" | custom-call | tf_op jit(solution)/shard_map/pallas_call | solution.py:261
  64.2 0.0 copy-start
  64.2 3.4 %copy.6 = f32[384,1536]{1,0:T(8,128)} copy(f32[384,1536]{1,0:T(8,128)} %get-tuple-element.4) | data formatting | bytes 4718592
  67.6 0.0 copy-done
  67.6 1.4 %copy.7 = f32[384,1536]{1,0:T(8,128)} copy(f32[384,1536]{1,0:T(8,128)S(1)} %copy-done) | data formatting | bytes 4718592
Async XLA Ops:
  64.2 3.4 %copy-start = (f32[384,1536]{1,0:T(8,128)S(1)}, f32[384,1536]{1,0:T(8,128)}, u32[]{:S(2)}) copy-start(f32[384,1536]{1,0:T(8,128)} %get-tuple-element.5) | copy-start | bytes 7077892

commit v10 on v9

--- a/solution.py
+++ b/solution.py
@@ -115,11 +115,6 @@
     row_start = r * rows
     col_start = c * cols
     n_chunks = rows // chunk
-    col_ids = col_start + lax.broadcasted_iota(jnp.int32, (chunk, cols), 1)
-
-    def diag_at(i0):
-        row_ids = row_start + i0 + lax.broadcasted_iota(jnp.int32, (chunk, cols), 0)
-        return row_ids == col_ids
 
     def record_top(i0, summed):
         first = jnp.max(summed, axis=1, keepdims=True)
@@ -146,16 +141,19 @@
             rowb_all[j * rb:(j + 1) * rb, :], colb_all, (((1,), (1,)), ((), ())),
             preferred_element_type=jnp.float32)
 
-    def sim_body(i, carry):
-        i0 = pl.multiple_of(i * chunk, chunk)
-        rq = rq_s[pl.ds(i0, chunk), 0:1]
-        dist = 2.0 * sim_s[pl.ds(i0, chunk), :] - rq - cq[...]
-        s = jnp.where(diag_at(i0), prefc[pl.ds(i0, chunk), 0:1], dist)
-        sim_s[pl.ds(i0, chunk), :] = s
-        record_top(i0, s)
-        return carry
-
-    lax.fori_loop(0, n_chunks, sim_body, 0)
+    has_diag = row_start // cols == c
+    band = pl.ds(pl.multiple_of(row_start % cols, rows), rows)
+
+    def eye():
+        return lax.broadcasted_iota(jnp.int32, (rows, rows), 0) == lax.broadcasted_iota(jnp.int32, (rows, rows), 1)
+
+    sim_s[...] = 2.0 * sim_s[...] - rq_s[:, 0:1] - cq[...]
+
+    @pl.when(has_diag)
+    def _():
+        sim_s[:, band] = jnp.where(eye(), prefc[:, 0:1], sim_s[:, band])
+
+    record_top(0, sim_s[...])
     for step in range(iters):
         first_step = step == 0
         last_step = step == iters - 1
@@ -186,23 +184,23 @@
         fcol[...] = jnp.broadcast_to(first, (128, rows)).T
         scol[...] = jnp.broadcast_to(second, (128, rows)).T
 
-        def resp_body(i, acc):
-            i0 = pl.multiple_of(i * chunk, chunk)
-            s = sim_s[pl.ds(i0, chunk), :]
-            summed = s if first_step else avail_prev[pl.ds(i0, chunk), :] + s
-            f = fcol[pl.ds(i0, chunk), 0:1]
-            sc = scol[pl.ds(i0, chunk), 0:1]
-            fresh = s - jnp.where(summed == f, sc, f)
-            if first_step:
-                resp = (1.0 - DAMPING) * fresh
-            else:
-                resp = DAMPING * resp_prev[pl.ds(i0, chunk), :] + (1.0 - DAMPING) * fresh
-            resp_new[pl.ds(i0, chunk), :] = resp
-            positive = jnp.where(diag_at(i0), resp, jnp.maximum(resp, 0.0))
-            return acc + jnp.sum(positive, axis=0, keepdims=True)
-
+        s = sim_s[...]
+        summed = s if first_step else avail_prev[...] + s
+        f = fcol[:, 0:1]
+        sc = scol[:, 0:1]
+        fresh = s - jnp.where(summed == f, sc, f)
+        if first_step:
+            resp = (1.0 - DAMPING) * fresh
+        else:
+            resp = DAMPING * resp_prev[...] + (1.0 - DAMPING) * fresh
+        resp_new[...] = resp
         zp = zpart.at[step]
-        zp[...] = lax.fori_loop(0, n_chunks, resp_body, jnp.zeros((1, cols), jnp.float32))
+        zp[...] = jnp.sum(jnp.maximum(resp, 0.0), axis=0, keepdims=True)
+
+        @pl.when(has_diag)
+        def _():
+            rb_ = resp_new[:, band]
+            zp[:, band] = jnp.sum(jnp.where(eye(), rb_, jnp.maximum(rb_, 0.0)), axis=0, keepdims=True)
 
         b1 = buf1.at[step]
         pltpu.make_async_copy(zp, b1.at[pl.ds(z, 1)], recv_z.at[step, z]).start()
@@ -228,23 +226,27 @@
             pltpu.make_async_copy(zs, b2.at[pl.ds(s, 1)], recv_y.at[step, s]).wait()
         colsum = jnp.sum(b2[...], axis=0, keepdims=True)
 
-        def avail_body(i, carry):
-            i0 = pl.multiple_of(i * chunk, chunk)
-            resp = resp_new[pl.ds(i0, chunk), :]
-            diag = diag_at(i0)
-            positive = jnp.where(diag, resp, jnp.maximum(resp, 0.0))
-            renew = colsum - positive
-            renew = jnp.where(diag, renew, jnp.minimum(renew, 0.0))
+        cq[...] = colsum
+        renew = jnp.minimum(colsum - jnp.maximum(resp_new[...], 0.0), 0.0)
+        if first_step:
+            avail_new[...] = (1.0 - DAMPING) * renew
+        else:
+            avail_new[...] = DAMPING * avail_prev[...] + (1.0 - DAMPING) * renew
+
+        @pl.when(has_diag)
+        def _():
+            rb_ = resp_new[:, band]
+            e = eye()
+            positive = jnp.where(e, rb_, jnp.maximum(rb_, 0.0))
+            renew_b = cq[:, band] - positive
+            renew_b = jnp.where(e, renew_b, jnp.minimum(renew_b, 0.0))
             if first_step:
-                avail = (1.0 - DAMPING) * renew
+                avail_new[:, band] = (1.0 - DAMPING) * renew_b
             else:
-                avail = DAMPING * avail_prev[pl.ds(i0, chunk), :] + (1.0 - DAMPING) * renew
-            avail_new[pl.ds(i0, chunk), :] = avail
-            if not last_step:
-                record_top(i0, avail + sim_s[pl.ds(i0, chunk), :])
-            return carry
-
-        lax.fori_loop(0, n_chunks, avail_body, 0)
+                avail_new[:, band] = DAMPING * avail_prev[:, band] + (1.0 - DAMPING) * renew_b
+
+        if not last_step:
+            record_top(0, avail_new[...] + sim_s[...])
     for cp in copies:
         cp.wait_send()
     for j, dev in enumerate(targets):

time: 69.1 us -> 68.4 us (0.990)
  Pallas kernels: 63.6 us -> 62.9 us
    pallas_call x1, Pallas kernels: 63.6 us -> 62.9 us  [propagate(): pl.pallas_call(functools.partial(ap_kernel, n_row, n_col, inner, rows, it...]
where the time goes in v10:
time: 68.4 us; the launch traced here: 68.3 us
  Pallas kernels  62.9 us (92%)
  local copies, waits for them, and re-layouts  4.78 us (7%)
    pallas_call x1, Pallas kernels, propagate(): pl.pallas_call(functools.partial(ap_kernel, n_row, n_col, inner, rows, it...  62.9 us
    unnamed x4, local copies, waits for them, and re-layouts  4.78 us

profile of v10, /device:TPU:2, one launch (start us, length us, event | category | flops | bytes accessed | tf_op | source)
XLA Modules:
  0.0 68.3 jit_solution(12687494874851978663)
XLA Ops:
  0.6 62.9 %shard_map.41 = (f32[384,1536]{1,0:T(8,128)}, f32[384,1536]{1,0:T(8,128)}) custom-call(bf16[48,256]{1,0:T(8,128)(2,1)} %bitcast.1, f32[384]{0:T(512)} %prefr_ref.1), custom_call_target="tpu_custom_call" | custom-call | tf_op jit(solution)/shard_map/pallas_call | solution.py:263
  63.5 0.0 copy-start
  63.5 3.4 %copy.6 = f32[384,1536]{1,0:T(8,128)} copy(f32[384,1536]{1,0:T(8,128)} %get-tuple-element.4) | data formatting | bytes 4718592
  66.9 0.0 copy-done
  66.9 1.4 %copy.7 = f32[384,1536]{1,0:T(8,128)} copy(f32[384,1536]{1,0:T(8,128)S(1)} %copy-done) | data formatting | bytes 4718592
Async XLA Ops:
  63.5 3.4 %copy-start = (f32[384,1536]{1,0:T(8,128)S(1)}, f32[384,1536]{1,0:T(8,128)}, u32[]{:S(2)}) copy-start(f32[384,1536]{1,0:T(8,128)} %get-tuple-element.5) | copy-start | bytes 7077892

commit v11 on v10

--- a/solution.py
+++ b/solution.py
@@ -262,7 +262,7 @@
     f32 = jnp.float32
     return pl.pallas_call(
         functools.partial(ap_kernel, n_row, n_col, inner, rows, iters),
-        out_shape=(jax.ShapeDtypeStruct((rows, cols), f32), jax.ShapeDtypeStruct((rows, cols), f32)),
+        out_shape=(pltpu.VMEM((rows, cols), f32), pltpu.VMEM((rows, cols), f32)),
         in_specs=[VMEM] * 2,
         out_specs=(VMEM, VMEM),
         scratch_shapes=[
@@ -297,7 +297,7 @@
             pltpu.SemaphoreType.DMA((iters, outer)),
         ],
         compiler_params=pltpu.CompilerParams(
-            collective_id=cid, has_side_effects=True, vmem_limit_bytes=60 * 1024 * 1024),
+            collective_id=cid, has_side_effects=True, vmem_limit_bytes=32 * 1024 * 1024),
     )(chunk, pref_row)
 
 

time: 68.4 us -> 65 us (0.950)
  Pallas kernels: 62.9 us -> 59.9 us
    pallas_call x1, Pallas kernels: 62.9 us -> 59.9 us  [propagate(): pl.pallas_call(functools.partial(ap_kernel, n_row, n_col, inner, rows, it...]
    unnamed x4 -> x6, local copies, waits for them, and re-layouts: 4.78 us -> 4.22 us
where the time goes in v11:
time: 65 us; the launch traced here: 64.8 us
  Pallas kernels  59.9 us (92%)
  local copies, waits for them, and re-layouts  4.22 us (6%)
  between operations  0.65 us (1%)
    pallas_call x1, Pallas kernels, propagate(): pl.pallas_call(functools.partial(ap_kernel, n_row, n_col, inner, rows, it...  59.9 us
    unnamed x6, local copies, waits for them, and re-layouts  4.22 us

profile of v11, /device:TPU:2, one launch (start us, length us, event | category | flops | bytes accessed | tf_op | source)
XLA Modules:
  0.0 64.8 jit_solution(2321976638364444166)
XLA Ops:
  0.6 0.0 copy-start
  0.6 0.7 %copy-done = bf16[1,1,48,256]{3,2,1,0:T(8,128)(2,1)S(1)} copy-done((bf16[1,1,48,256]{3,2,1,0:T(8,128)(2,1)S(1)}, bf16[1,1,48,256]{3,2,1,0:T(8,128)(2,1)}, u32[]{:S(2)}) %copy-start) | copy-done | bytes 24600
  1.4 0.0 copy-start.1
  1.4 0.7 %copy-done.1 = f32[384]{0:T(512)S(1)} copy-done((f32[384]{0:T(512)S(1)}, f32[384]{0:T(512)}, u32[]{:S(2)}) %copy-start.1) | copy-done | bytes 1560
  2.0 59.9 %shard_map.41 = (f32[384,1536]{1,0:T(8,128)S(1)}, f32[384,1536]{1,0:T(8,128)S(1)}) custom-call(bf16[48,256]{1,0:T(8,128)(2,1)S(1)} %bitcast.1, f32[384]{0:T(512)S(1)} %copy-done.1), custom_call_target="tpu_custom_call" | custom-call | tf_op jit(solution)/shard_map/pallas_call | solution.py:263
  62.0 1.4 %copy.6 = f32[384,1536]{1,0:T(8,128)} copy(f32[384,1536]{1,0:T(8,128)S(1)} %get-tuple-element.2) | data formatting | bytes 4718592
  63.4 1.4 %copy.7 = f32[384,1536]{1,0:T(8,128)} copy(f32[384,1536]{1,0:T(8,128)S(1)} %get-tuple-element.3) | data formatting | bytes 4718592
Async XLA Ops:
  0.6 0.7 %copy-start = (bf16[1,1,48,256]{3,2,1,0:T(8,128)(2,1)S(1)}, bf16[1,1,48,256]{3,2,1,0:T(8,128)(2,1)}, u32[]{:S(2)}) copy-start(bf16[1,1,48,256]{3,2,1,0:T(8,128)(2,1)} %param.2) | copy-start | bytes 73732
  1.4 0.7 %copy-start.1 = (f32[384]{0:T(512)S(1)}, f32[384]{0:T(512)}, u32[]{:S(2)}) copy-start(f32[384]{0:T(512)} %prefr_ref.1) | copy-start | bytes 4612

commit v12 on v11

--- a/solution.py
+++ b/solution.py
@@ -162,20 +162,18 @@
         pk = pack.at[step]
         pk[0:1, :] = fcol[...].T[0:1, :]
         pk[1:2, :] = scol[...].T[0:1, :]
-        for k, dst in enumerate((buf_f.at[step], buf_s.at[step])):
-            src = pk.at[pl.ds(k, 1)]
-            pltpu.make_async_copy(src, dst.at[pl.ds(c, 1)], recv_t.at[step, k, c]).start()
-            for i, p in enumerate(cpeers):
-                cp = pltpu.make_async_remote_copy(
-                    src_ref=src, dst_ref=dst.at[pl.ds(c, 1)], send_sem=send_t.at[step, k, i],
-                    recv_sem=recv_t.at[step, k, c], device_id={"col": p}, device_id_type=MESH)
-                cp.start()
-                copies.append(cp)
-        for k, dst in enumerate((buf_f.at[step], buf_s.at[step])):
-            for s in range(n_col):
-                pltpu.make_async_copy(pk.at[pl.ds(0, 1)], dst.at[pl.ds(s, 1)], recv_t.at[step, k, s]).wait()
-        firsts = buf_f[step]
-        seconds = buf_s[step]
+        dst = buf_f.at[step]
+        pltpu.make_async_copy(pk, dst.at[c], recv_t.at[step, 0, c]).start()
+        for i, p in enumerate(cpeers):
+            cp = pltpu.make_async_remote_copy(
+                src_ref=pk, dst_ref=dst.at[c], send_sem=send_t.at[step, 0, i],
+                recv_sem=recv_t.at[step, 0, c], device_id={"col": p}, device_id_type=MESH)
+            cp.start()
+            copies.append(cp)
+        for s in range(n_col):
+            pltpu.make_async_copy(pk, dst.at[s], recv_t.at[step, 0, s]).wait()
+        firsts = dst[:, 0, :]
+        seconds = dst[:, 1, :]
         first = jnp.max(firsts, axis=0, keepdims=True)
         at_top = firsts == first
         repeats = jnp.sum(at_top.astype(jnp.float32), axis=0, keepdims=True)
@@ -276,7 +274,7 @@
             pltpu.VMEM((rows, 128), f32),
             pltpu.VMEM((1, cols), f32),
             pltpu.VMEM((iters, 2, rows), f32),
-            pltpu.VMEM((iters, n_col, rows), f32),
+            pltpu.VMEM((iters, n_col, 2, rows), f32),
             pltpu.VMEM((iters, n_col, rows), f32),
             pltpu.VMEM((iters, 1, cols), f32),
             pltpu.VMEM((iters, inner, cols), f32),

time: 65 us -> 64.9 us (level)
  no operation moved by 1% of the time
where the time goes in v12:
time: 64.9 us; the launch traced here: 64.7 us
  Pallas kernels  59.8 us (92%)
  local copies, waits for them, and re-layouts  4.22 us (7%)
  between operations  0.65 us (1%)
    pallas_call x1, Pallas kernels, propagate(): pl.pallas_call(functools.partial(ap_kernel, n_row, n_col, inner, rows, it...  59.8 us
    unnamed x6, local copies, waits for them, and re-layouts  4.22 us

profile of v12, /device:TPU:2, one launch (start us, length us, event | category | flops | bytes accessed | tf_op | source)
XLA Modules:
  0.0 64.7 jit_solution(6093663485588640569)
XLA Ops:
  0.6 0.0 copy-start
  0.6 0.7 %copy-done = bf16[1,1,48,256]{3,2,1,0:T(8,128)(2,1)S(1)} copy-done((bf16[1,1,48,256]{3,2,1,0:T(8,128)(2,1)S(1)}, bf16[1,1,48,256]{3,2,1,0:T(8,128)(2,1)}, u32[]{:S(2)}) %copy-start) | copy-done | bytes 24600
  1.4 0.0 copy-start.1
  1.4 0.7 %copy-done.1 = f32[384]{0:T(512)S(1)} copy-done((f32[384]{0:T(512)S(1)}, f32[384]{0:T(512)}, u32[]{:S(2)}) %copy-start.1) | copy-done | bytes 1560
  2.0 59.8 %shard_map.41 = (f32[384,1536]{1,0:T(8,128)S(1)}, f32[384,1536]{1,0:T(8,128)S(1)}) custom-call(bf16[48,256]{1,0:T(8,128)(2,1)S(1)} %bitcast.1, f32[384]{0:T(512)S(1)} %copy-done.1), custom_call_target="tpu_custom_call" | custom-call | tf_op jit(solution)/shard_map/pallas_call | solution.py:261
  61.9 1.4 %copy.6 = f32[384,1536]{1,0:T(8,128)} copy(f32[384,1536]{1,0:T(8,128)S(1)} %get-tuple-element.2) | data formatting | bytes 4718592
  63.3 1.4 %copy.7 = f32[384,1536]{1,0:T(8,128)} copy(f32[384,1536]{1,0:T(8,128)S(1)} %get-tuple-element.3) | data formatting | bytes 4718592
Async XLA Ops:
  0.6 0.7 %copy-start = (bf16[1,1,48,256]{3,2,1,0:T(8,128)(2,1)S(1)}, bf16[1,1,48,256]{3,2,1,0:T(8,128)(2,1)}, u32[]{:S(2)}) copy-start(bf16[1,1,48,256]{3,2,1,0:T(8,128)(2,1)} %param.2) | copy-start | bytes 73732
  1.4 0.7 %copy-start.1 = (f32[384]{0:T(512)S(1)}, f32[384]{0:T(512)}, u32[]{:S(2)}) copy-start(f32[384]{0:T(512)} %prefr_ref.1) | copy-start | bytes 4612

commit v13 on v11

--- a/solution.py
+++ b/solution.py
@@ -91,11 +91,6 @@
                 recv_sem=e_recv_b.at[y, zs], device_id={"row": p}, device_id_type=MESH)
             cp.start()
             copies.append(cp)
-    for d in range(1, outer):
-        yo = lax.rem(y + d, outer)
-        for s in range(inner):
-            other = colb3.at[yo * inner + s]
-            pltpu.make_async_copy(other, other, e_recv_b.at[yo, s]).wait()
     for t in range(n_col // 2):
         s = 2 * t + parity
         pltpu.make_async_copy(chunk_ref, rowb3.at[s], e_recv_r.at[s]).wait()
@@ -125,21 +120,24 @@
         fcol[pl.ds(i0, chunk), :] = jnp.broadcast_to(first, (chunk, 128))
         scol[pl.ds(i0, chunk), :] = jnp.broadcast_to(second, (chunk, 128))
 
-    colb_all = colb_ref[...].reshape(cols, -1)
     rowb_all = rowb_ref[...].reshape(rows, -1)
-    cb = 128 if cols % 128 == 0 else cols
-    for j in range(cols // cb):
-        xc = colb_all[j * cb:(j + 1) * cb, :].astype(jnp.float32)
-        qc = jnp.sum(xc * xc, axis=1, keepdims=True)
-        cq[0:1, pl.ds(j * cb, cb)] = jnp.broadcast_to(qc, (cb, 128)).T[0:1, :]
     xr = rowb_all.astype(jnp.float32)
     rq_s = fcol
     rq_s[...] = jnp.broadcast_to(jnp.sum(xr * xr, axis=1, keepdims=True), (rows, 128))
-    rb = 128 if rows % 128 == 0 else rows
-    for j in range(rows // rb):
-        sim_s[pl.ds(j * rb, rb), :] = lax.dot_general(
-            rowb_all[j * rb:(j + 1) * rb, :], colb_all, (((1,), (1,)), ((), ())),
-            preferred_element_type=jnp.float32)
+    blk = inner * mol
+    for d in range(outer):
+        yo = lax.rem(y + d, outer)
+        if d > 0:
+            for s in range(inner):
+                other = colb3.at[yo * inner + s]
+                pltpu.make_async_copy(other, other, e_recv_b.at[yo, s]).wait()
+        xb = colb_ref[pl.ds(yo * inner, inner)].reshape(blk, -1)
+        xc = xb.astype(jnp.float32)
+        qc = jnp.sum(xc * xc, axis=1, keepdims=True)
+        cols_at = pl.ds(pl.multiple_of(yo * blk, blk), blk)
+        cq[:, cols_at] = jnp.broadcast_to(qc, (blk, 128)).T[0:1, :]
+        sim_s[:, cols_at] = lax.dot_general(
+            rowb_all, xb, (((1,), (1,)), ((), ())), preferred_element_type=jnp.float32)
 
     has_diag = row_start // cols == c
     band = pl.ds(pl.multiple_of(row_start % cols, rows), rows)

time: 65 us -> 64.3 us (0.989)
    pallas_call x1, Pallas kernels: 59.9 us -> 59.3 us  [propagate(): pl.pallas_call(functools.partial(ap_kernel, n_row, n_col, inner, rows, it...]
where the time goes in v13:
time: 64.3 us; the launch traced here: 64.1 us
  Pallas kernels  59.3 us (92%)
  local copies, waits for them, and re-layouts  4.22 us (7%)
  between operations  0.65 us (1%)
    pallas_call x1, Pallas kernels, propagate(): pl.pallas_call(functools.partial(ap_kernel, n_row, n_col, inner, rows, it...  59.3 us
    unnamed x6, local copies, waits for them, and re-layouts  4.22 us

profile of v13, /device:TPU:2, one launch (start us, length us, event | category | flops | bytes accessed | tf_op | source)
XLA Modules:
  0.0 64.1 jit_solution(17227596039354637986)
XLA Ops:
  0.6 0.0 copy-start
  0.6 0.7 %copy-done = bf16[1,1,48,256]{3,2,1,0:T(8,128)(2,1)S(1)} copy-done((bf16[1,1,48,256]{3,2,1,0:T(8,128)(2,1)S(1)}, bf16[1,1,48,256]{3,2,1,0:T(8,128)(2,1)}, u32[]{:S(2)}) %copy-start) | copy-done | bytes 24600
  1.4 0.0 copy-start.1
  1.4 0.7 %copy-done.1 = f32[384]{0:T(512)S(1)} copy-done((f32[384]{0:T(512)S(1)}, f32[384]{0:T(512)}, u32[]{:S(2)}) %copy-start.1) | copy-done | bytes 1560
  2.0 59.3 %shard_map.41 = (f32[384,1536]{1,0:T(8,128)S(1)}, f32[384,1536]{1,0:T(8,128)S(1)}) custom-call(bf16[48,256]{1,0:T(8,128)(2,1)S(1)} %bitcast.1, f32[384]{0:T(512)S(1)} %copy-done.1), custom_call_target="tpu_custom_call" | custom-call | tf_op jit(solution)/shard_map/pallas_call | solution.py:261
  61.3 1.4 %copy.6 = f32[384,1536]{1,0:T(8,128)} copy(f32[384,1536]{1,0:T(8,128)S(1)} %get-tuple-element.2) | data formatting | bytes 4718592
  62.7 1.4 %copy.7 = f32[384,1536]{1,0:T(8,128)} copy(f32[384,1536]{1,0:T(8,128)S(1)} %get-tuple-element.3) | data formatting | bytes 4718592
Async XLA Ops:
  0.6 0.7 %copy-start = (bf16[1,1,48,256]{3,2,1,0:T(8,128)(2,1)S(1)}, bf16[1,1,48,256]{3,2,1,0:T(8,128)(2,1)}, u32[]{:S(2)}) copy-start(bf16[1,1,48,256]{3,2,1,0:T(8,128)(2,1)} %param.2) | copy-start | bytes 73732
  1.4 0.7 %copy-start.1 = (f32[384]{0:T(512)S(1)}, f32[384]{0:T(512)}, u32[]{:S(2)}) copy-start(f32[384]{0:T(512)} %prefr_ref.1) | copy-start | bytes 4612

commit v14 on v13

--- a/solution.py
+++ b/solution.py
@@ -103,13 +103,11 @@
         s = 2 * t + 1 - parity
         pltpu.make_async_copy(chunk_ref, rowb3.at[s], e_recv_r.at[s]).wait()
     mol = chunk_ref.shape[0]
+    row_start = r * rows
+    col_start = c * cols
     colb_ref = colb3
     rowb_ref = rowb3
 
-
-    row_start = r * rows
-    col_start = c * cols
-    n_chunks = rows // chunk
 
     def record_top(i0, summed):
         first = jnp.max(summed, axis=1, keepdims=True)
@@ -125,6 +123,7 @@
     rq_s = fcol
     rq_s[...] = jnp.broadcast_to(jnp.sum(xr * xr, axis=1, keepdims=True), (rows, 128))
     blk = inner * mol
+    block_firsts, block_seconds = [], []
     for d in range(outer):
         yo = lax.rem(y + d, outer)
         if d > 0:
@@ -136,22 +135,37 @@
         qc = jnp.sum(xc * xc, axis=1, keepdims=True)
         cols_at = pl.ds(pl.multiple_of(yo * blk, blk), blk)
         cq[:, cols_at] = jnp.broadcast_to(qc, (blk, 128)).T[0:1, :]
-        sim_s[:, cols_at] = lax.dot_general(
+        cross = lax.dot_general(
             rowb_all, xb, (((1,), (1,)), ((), ())), preferred_element_type=jnp.float32)
+        sim_s[:, cols_at] = 2.0 * cross - rq_s[:, 0:1] - cq[:, cols_at]
+        block_start = col_start + yo * blk
+
+        @pl.when(jnp.logical_and(row_start < block_start + blk, block_start < row_start + rows))
+        def _():
+            row_ids = row_start + lax.broadcasted_iota(jnp.int32, (rows, blk), 0)
+            col_ids = block_start + lax.broadcasted_iota(jnp.int32, (rows, blk), 1)
+            sim_s[:, cols_at] = jnp.where(row_ids == col_ids, prefc[:, 0:1], sim_s[:, cols_at])
+
+        summed = sim_s[:, cols_at]
+        first = jnp.max(summed, axis=1, keepdims=True)
+        hits = summed == first
+        repeats = jnp.sum(hits.astype(jnp.float32), axis=1, keepdims=True)
+        others = jnp.max(jnp.where(hits, -jnp.inf, summed), axis=1, keepdims=True)
+        block_firsts.append(first)
+        block_seconds.append(jnp.where(repeats > 1.0, first, others))
+
+    first = functools.reduce(jnp.maximum, block_firsts)
+    repeats = functools.reduce(jnp.add, [(f == first).astype(jnp.float32) for f in block_firsts])
+    others = functools.reduce(jnp.maximum, [jnp.where(f == first, -jnp.inf, f) for f in block_firsts])
+    second = jnp.where(repeats > 1.0, first, jnp.maximum(functools.reduce(jnp.maximum, block_seconds), others))
+    fcol[...] = jnp.broadcast_to(first, (rows, 128))
+    scol[...] = jnp.broadcast_to(second, (rows, 128))
 
     has_diag = row_start // cols == c
     band = pl.ds(pl.multiple_of(row_start % cols, rows), rows)
 
     def eye():
         return lax.broadcasted_iota(jnp.int32, (rows, rows), 0) == lax.broadcasted_iota(jnp.int32, (rows, rows), 1)
-
-    sim_s[...] = 2.0 * sim_s[...] - rq_s[:, 0:1] - cq[...]
-
-    @pl.when(has_diag)
-    def _():
-        sim_s[:, band] = jnp.where(eye(), prefc[:, 0:1], sim_s[:, band])
-
-    record_top(0, sim_s[...])
     for step in range(iters):
         first_step = step == 0
         last_step = step == iters - 1

time: 64.3 us -> 63.9 us (level)
  no operation moved by 1% of the time
where the time goes in v14:
time: 63.9 us; the launch traced here: 63.7 us
  Pallas kernels  58.8 us (92%)
  local copies, waits for them, and re-layouts  4.22 us (7%)
  between operations  0.65 us (1%)
    pallas_call x1, Pallas kernels, propagate(): pl.pallas_call(functools.partial(ap_kernel, n_row, n_col, inner, rows, it...  58.8 us
    unnamed x6, local copies, waits for them, and re-layouts  4.22 us

profile of v14, /device:TPU:2, one launch (start us, length us, event | category | flops | bytes accessed | tf_op | source)
XLA Modules:
  0.0 63.7 jit_solution(18034166707700909632)
XLA Ops:
  0.6 0.0 copy-start
  0.6 0.7 %copy-done = bf16[1,1,48,256]{3,2,1,0:T(8,128)(2,1)S(1)} copy-done((bf16[1,1,48,256]{3,2,1,0:T(8,128)(2,1)S(1)}, bf16[1,1,48,256]{3,2,1,0:T(8,128)(2,1)}, u32[]{:S(2)}) %copy-start) | copy-done | bytes 24600
  1.4 0.0 copy-start.1
  1.4 0.7 %copy-done.1 = f32[384]{0:T(512)S(1)} copy-done((f32[384]{0:T(512)S(1)}, f32[384]{0:T(512)}, u32[]{:S(2)}) %copy-start.1) | copy-done | bytes 1560
  2.0 58.8 %shard_map.41 = (f32[384,1536]{1,0:T(8,128)S(1)}, f32[384,1536]{1,0:T(8,128)S(1)}) custom-call(bf16[48,256]{1,0:T(8,128)(2,1)S(1)} %bitcast.1, f32[384]{0:T(512)S(1)} %copy-done.1), custom_call_target="tpu_custom_call" | custom-call | tf_op jit(solution)/shard_map/pallas_call | solution.py:275
  60.9 1.4 %copy.6 = f32[384,1536]{1,0:T(8,128)} copy(f32[384,1536]{1,0:T(8,128)S(1)} %get-tuple-element.2) | data formatting | bytes 4718592
  62.3 1.4 %copy.7 = f32[384,1536]{1,0:T(8,128)} copy(f32[384,1536]{1,0:T(8,128)S(1)} %get-tuple-element.3) | data formatting | bytes 4718592
Async XLA Ops:
  0.6 0.7 %copy-start = (bf16[1,1,48,256]{3,2,1,0:T(8,128)(2,1)S(1)}, bf16[1,1,48,256]{3,2,1,0:T(8,128)(2,1)}, u32[]{:S(2)}) copy-start(bf16[1,1,48,256]{3,2,1,0:T(8,128)(2,1)} %param.2) | copy-start | bytes 73732
  1.4 0.7 %copy-start.1 = (f32[384]{0:T(512)S(1)}, f32[384]{0:T(512)}, u32[]{:S(2)}) copy-start(f32[384]{0:T(512)} %prefr_ref.1) | copy-start | bytes 4612

commit v15 on v14

--- a/solution.py
+++ b/solution.py
@@ -196,34 +196,44 @@
         fcol[...] = jnp.broadcast_to(first, (128, rows)).T
         scol[...] = jnp.broadcast_to(second, (128, rows)).T
 
-        s = sim_s[...]
-        summed = s if first_step else avail_prev[...] + s
-        f = fcol[:, 0:1]
-        sc = scol[:, 0:1]
-        fresh = s - jnp.where(summed == f, sc, f)
-        if first_step:
-            resp = (1.0 - DAMPING) * fresh
-        else:
-            resp = DAMPING * resp_prev[...] + (1.0 - DAMPING) * fresh
-        resp_new[...] = resp
         zp = zpart.at[step]
-        zp[...] = jnp.sum(jnp.maximum(resp, 0.0), axis=0, keepdims=True)
-
-        @pl.when(has_diag)
-        def _():
-            rb_ = resp_new[:, band]
-            zp[:, band] = jnp.sum(jnp.where(eye(), rb_, jnp.maximum(rb_, 0.0)), axis=0, keepdims=True)
-
         b1 = buf1.at[step]
-        pltpu.make_async_copy(zp, b1.at[pl.ds(z, 1)], recv_z.at[step, z]).start()
-        for i, p in enumerate(zpeers):
-            cp = pltpu.make_async_remote_copy(
-                src_ref=zp, dst_ref=b1.at[pl.ds(z, 1)], send_sem=send_z.at[step, i],
-                recv_sem=recv_z.at[step, z], device_id={"row": p}, device_id_type=MESH)
-            cp.start()
-            copies.append(cp)
-        for s in range(inner):
-            pltpu.make_async_copy(zp, b1.at[pl.ds(s, 1)], recv_z.at[step, s]).wait()
+        half = cols // 2
+        for h in range(2):
+            hc = pl.ds(h * half, half)
+            s = sim_s[:, hc]
+            summed = s if first_step else avail_prev[:, hc] + s
+            f = fcol[:, 0:1]
+            sc = scol[:, 0:1]
+            fresh = s - jnp.where(summed == f, sc, f)
+            if first_step:
+                resp = (1.0 - DAMPING) * fresh
+            else:
+                resp = DAMPING * resp_prev[:, hc] + (1.0 - DAMPING) * fresh
+            resp_new[:, hc] = resp
+            zp[:, hc] = jnp.sum(jnp.maximum(resp, 0.0), axis=0, keepdims=True)
+            h_start = col_start + h * half
+
+            @pl.when(jnp.logical_and(row_start < h_start + half, h_start < row_start + rows))
+            def _():
+                row_ids = row_start + lax.broadcasted_iota(jnp.int32, (rows, half), 0)
+                col_ids = h_start + lax.broadcasted_iota(jnp.int32, (rows, half), 1)
+                rh = resp_new[:, hc]
+                zp[:, hc] = jnp.sum(jnp.where(row_ids == col_ids, rh, jnp.maximum(rh, 0.0)), axis=0, keepdims=True)
+
+            src_h = zp.at[:, hc]
+            dst_h = b1.at[pl.ds(z, 1), hc]
+            pltpu.make_async_copy(src_h, dst_h, recv_z.at[step, h, z]).start()
+            for i, p in enumerate(zpeers):
+                cp = pltpu.make_async_remote_copy(
+                    src_ref=src_h, dst_ref=dst_h, send_sem=send_z.at[step, h, i],
+                    recv_sem=recv_z.at[step, h, z], device_id={"row": p}, device_id_type=MESH)
+                cp.start()
+                copies.append(cp)
+        for h in range(2):
+            hc = pl.ds(h * half, half)
+            for s in range(inner):
+                pltpu.make_async_copy(zp.at[:, hc], b1.at[pl.ds(s, 1), hc], recv_z.at[step, h, s]).wait()
         zs = zsum.at[step]
         zs[...] = jnp.sum(b1[...], axis=0, keepdims=True)
         b2 = buf2.at[step]
@@ -303,9 +313,9 @@
             pltpu.SemaphoreType.DMA((n_col,)),
             pltpu.SemaphoreType.DMA((iters, 2, n_col - 1)),
             pltpu.SemaphoreType.DMA((iters, 2, n_col)),
-            pltpu.SemaphoreType.DMA((iters, inner - 1)),
+            pltpu.SemaphoreType.DMA((iters, 2, inner - 1)),
             pltpu.SemaphoreType.DMA((iters, outer - 1)),
-            pltpu.SemaphoreType.DMA((iters, inner)),
+            pltpu.SemaphoreType.DMA((iters, 2, inner)),
             pltpu.SemaphoreType.DMA((iters, outer)),
         ],
         compiler_params=pltpu.CompilerParams(

time: 63.9 us -> 64.4 us (level)
  no operation moved by 1% of the time
where the time goes in v15:
time: 64.4 us; the launch traced here: 63.9 us
  Pallas kernels  59 us (92%)
  local copies, waits for them, and re-layouts  4.22 us (7%)
  between operations  0.65 us (1%)
    pallas_call x1, Pallas kernels, propagate(): pl.pallas_call(functools.partial(ap_kernel, n_row, n_col, inner, rows, it...  59 us
    unnamed x6, local copies, waits for them, and re-layouts  4.22 us

profile of v15, /device:TPU:2, one launch (start us, length us, event | category | flops | bytes accessed | tf_op | source)
XLA Modules:
  0.0 63.9 jit_solution(1114861195192931546)
XLA Ops:
  0.6 0.0 copy-start
  0.6 0.7 %copy-done = bf16[1,1,48,256]{3,2,1,0:T(8,128)(2,1)S(1)} copy-done((bf16[1,1,48,256]{3,2,1,0:T(8,128)(2,1)S(1)}, bf16[1,1,48,256]{3,2,1,0:T(8,128)(2,1)}, u32[]{:S(2)}) %copy-start) | copy-done | bytes 24600
  1.4 0.0 copy-start.1
  1.4 0.7 %copy-done.1 = f32[384]{0:T(512)S(1)} copy-done((f32[384]{0:T(512)S(1)}, f32[384]{0:T(512)}, u32[]{:S(2)}) %copy-start.1) | copy-done | bytes 1560
  2.0 59.0 %shard_map.41 = (f32[384,1536]{1,0:T(8,128)S(1)}, f32[384,1536]{1,0:T(8,128)S(1)}) custom-call(bf16[48,256]{1,0:T(8,128)(2,1)S(1)} %bitcast.1, f32[384]{0:T(512)S(1)} %copy-done.1), custom_call_target="tpu_custom_call" | custom-call | tf_op jit(solution)/shard_map/pallas_call | solution.py:285
  61.1 1.4 %copy.6 = f32[384,1536]{1,0:T(8,128)} copy(f32[384,1536]{1,0:T(8,128)S(1)} %get-tuple-element.2) | data formatting | bytes 4718592
  62.5 1.4 %copy.7 = f32[384,1536]{1,0:T(8,128)} copy(f32[384,1536]{1,0:T(8,128)S(1)} %get-tuple-element.3) | data formatting | bytes 4718592
Async XLA Ops:
  0.6 0.7 %copy-start = (bf16[1,1,48,256]{3,2,1,0:T(8,128)(2,1)S(1)}, bf16[1,1,48,256]{3,2,1,0:T(8,128)(2,1)}, u32[]{:S(2)}) copy-start(bf16[1,1,48,256]{3,2,1,0:T(8,128)(2,1)} %param.2) | copy-start | bytes 73732
  1.4 0.7 %copy-start.1 = (f32[384]{0:T(512)S(1)}, f32[384]{0:T(512)}, u32[]{:S(2)}) copy-start(f32[384]{0:T(512)} %prefr_ref.1) | copy-start | bytes 4612

commit v16 on v14

--- a/solution.py
+++ b/solution.py
@@ -239,6 +239,45 @@
         colsum = jnp.sum(b2[...], axis=0, keepdims=True)
 
         cq[...] = colsum
+        if not last_step:
+            b_firsts, b_seconds = [], []
+            for b in range(cols // blk):
+                bc = pl.ds(b * blk, blk)
+                rb_ = resp_new[:, bc]
+                renew = jnp.minimum(cq[:, bc] - jnp.maximum(rb_, 0.0), 0.0)
+                if first_step:
+                    avail_new[:, bc] = (1.0 - DAMPING) * renew
+                else:
+                    avail_new[:, bc] = DAMPING * avail_prev[:, bc] + (1.0 - DAMPING) * renew
+                b_start = col_start + b * blk
+
+                @pl.when(jnp.logical_and(row_start < b_start + blk, b_start < row_start + rows))
+                def _():
+                    row_ids = row_start + lax.broadcasted_iota(jnp.int32, (rows, blk), 0)
+                    col_ids = b_start + lax.broadcasted_iota(jnp.int32, (rows, blk), 1)
+                    diag = row_ids == col_ids
+                    rd = resp_new[:, bc]
+                    renew_b = cq[:, bc] - jnp.where(diag, rd, jnp.maximum(rd, 0.0))
+                    renew_b = jnp.where(diag, renew_b, jnp.minimum(renew_b, 0.0))
+                    if first_step:
+                        avail_new[:, bc] = (1.0 - DAMPING) * renew_b
+                    else:
+                        avail_new[:, bc] = DAMPING * avail_prev[:, bc] + (1.0 - DAMPING) * renew_b
+
+                summed = avail_new[:, bc] + sim_s[:, bc]
+                bf = jnp.max(summed, axis=1, keepdims=True)
+                hits = summed == bf
+                reps = jnp.sum(hits.astype(jnp.float32), axis=1, keepdims=True)
+                oth = jnp.max(jnp.where(hits, -jnp.inf, summed), axis=1, keepdims=True)
+                b_firsts.append(bf)
+                b_seconds.append(jnp.where(reps > 1.0, bf, oth))
+            fm = functools.reduce(jnp.maximum, b_firsts)
+            reps = functools.reduce(jnp.add, [(v == fm).astype(jnp.float32) for v in b_firsts])
+            oth = functools.reduce(jnp.maximum, [jnp.where(v == fm, -jnp.inf, v) for v in b_firsts])
+            sm = jnp.where(reps > 1.0, fm, jnp.maximum(functools.reduce(jnp.maximum, b_seconds), oth))
+            fcol[...] = jnp.broadcast_to(fm, (rows, 128))
+            scol[...] = jnp.broadcast_to(sm, (rows, 128))
+            continue
         renew = jnp.minimum(colsum - jnp.maximum(resp_new[...], 0.0), 0.0)
         if first_step:
             avail_new[...] = (1.0 - DAMPING) * renew

time: 63.9 us -> 64.3 us (level)
  no operation moved by 1% of the time
where the time goes in v16:
time: 64.3 us; the launch traced here: 64.1 us
  Pallas kernels  59.2 us (92%)
  local copies, waits for them, and re-layouts  4.22 us (7%)
  between operations  0.65 us (1%)
    pallas_call x1, Pallas kernels, propagate(): pl.pallas_call(functools.partial(ap_kernel, n_row, n_col, inner, rows, it...  59.2 us
    unnamed x6, local copies, waits for them, and re-layouts  4.22 us

profile of v16, /device:TPU:2, one launch (start us, length us, event | category | flops | bytes accessed | tf_op | source)
XLA Modules:
  0.0 64.1 jit_solution(14245096023765231346)
XLA Ops:
  0.6 0.0 copy-start
  0.6 0.7 %copy-done = bf16[1,1,48,256]{3,2,1,0:T(8,128)(2,1)S(1)} copy-done((bf16[1,1,48,256]{3,2,1,0:T(8,128)(2,1)S(1)}, bf16[1,1,48,256]{3,2,1,0:T(8,128)(2,1)}, u32[]{:S(2)}) %copy-start) | copy-done | bytes 24600
  1.4 0.0 copy-start.1
  1.4 0.7 %copy-done.1 = f32[384]{0:T(512)S(1)} copy-done((f32[384]{0:T(512)S(1)}, f32[384]{0:T(512)}, u32[]{:S(2)}) %copy-start.1) | copy-done | bytes 1560
  2.0 59.2 %shard_map.41 = (f32[384,1536]{1,0:T(8,128)S(1)}, f32[384,1536]{1,0:T(8,128)S(1)}) custom-call(bf16[48,256]{1,0:T(8,128)(2,1)S(1)} %bitcast.1, f32[384]{0:T(512)S(1)} %copy-done.1), custom_call_target="tpu_custom_call" | custom-call | tf_op jit(solution)/shard_map/pallas_call | solution.py:314
  61.3 1.4 %copy.6 = f32[384,1536]{1,0:T(8,128)} copy(f32[384,1536]{1,0:T(8,128)S(1)} %get-tuple-element.2) | data formatting | bytes 4718592
  62.7 1.4 %copy.7 = f32[384,1536]{1,0:T(8,128)} copy(f32[384,1536]{1,0:T(8,128)S(1)} %get-tuple-element.3) | data formatting | bytes 4718592
Async XLA Ops:
  0.6 0.7 %copy-start = (bf16[1,1,48,256]{3,2,1,0:T(8,128)(2,1)S(1)}, bf16[1,1,48,256]{3,2,1,0:T(8,128)(2,1)}, u32[]{:S(2)}) copy-start(bf16[1,1,48,256]{3,2,1,0:T(8,128)(2,1)} %param.2) | copy-start | bytes 73732
  1.4 0.7 %copy-start.1 = (f32[384]{0:T(512)S(1)}, f32[384]{0:T(512)}, u32[]{:S(2)}) copy-start(f32[384]{0:T(512)} %prefr_ref.1) | copy-start | bytes 4612

commit v17 on v14

--- a/solution.py
+++ b/solution.py
@@ -55,10 +55,11 @@
         def _():
             pl.semaphore_signal(barrier, inc=1, device_id=dev, device_id_type=MESH)
     self_in = jnp.logical_and(target_row == r, my_slot % 2 == parity).astype(jnp.int32)
+    pltpu.make_async_copy(chunk_ref, colb3.at[r], e_recv_c.at[z]).start()
+    prefc[...] = jnp.broadcast_to(prefr_ref[...].reshape(1, rows), (128, rows)).T
     pl.semaphore_wait(barrier, (n_col - 1) + (inner - 1) + (outer - 1) + 2 * (n_col // 2 - self_in))
 
     copies = []
-    pltpu.make_async_copy(chunk_ref, colb3.at[r], e_recv_c.at[z]).start()
     for i, p in enumerate(zpeers):
         cp = pltpu.make_async_remote_copy(
             src_ref=chunk_ref, dst_ref=colb3.at[r], send_sem=e_send_z.at[i],
@@ -80,7 +81,6 @@
         def _():
             pltpu.make_async_copy(chunk_ref, rowb3.at[my_slot], e_recv_r.at[my_slot]).start()
 
-    prefc[...] = jnp.broadcast_to(prefr_ref[...].reshape(1, rows), (128, rows)).T
     for d in range(inner):
         zs = lax.rem(z + d, inner)
         slot = colb3.at[y * inner + zs]

time: 63.9 us -> 63.9 us (level)
  no operation moved by 1% of the time
where the time goes in v17:
time: 63.9 us; the launch traced here: 63.7 us
  Pallas kernels  58.8 us (92%)
  local copies, waits for them, and re-layouts  4.22 us (7%)
  between operations  0.65 us (1%)
    pallas_call x1, Pallas kernels, propagate(): pl.pallas_call(functools.partial(ap_kernel, n_row, n_col, inner, rows, it...  58.8 us
    unnamed x6, local copies, waits for them, and re-layouts  4.22 us

profile of v17, /device:TPU:2, one launch (start us, length us, event | category | flops | bytes accessed | tf_op | source)
XLA Modules:
  0.0 63.7 jit_solution(10849153834143822888)
XLA Ops:
  0.6 0.0 copy-start
  0.6 0.7 %copy-done = bf16[1,1,48,256]{3,2,1,0:T(8,128)(2,1)S(1)} copy-done((bf16[1,1,48,256]{3,2,1,0:T(8,128)(2,1)S(1)}, bf16[1,1,48,256]{3,2,1,0:T(8,128)(2,1)}, u32[]{:S(2)}) %copy-start) | copy-done | bytes 24600
  1.4 0.0 copy-start.1
  1.4 0.7 %copy-done.1 = f32[384]{0:T(512)S(1)} copy-done((f32[384]{0:T(512)S(1)}, f32[384]{0:T(512)}, u32[]{:S(2)}) %copy-start.1) | copy-done | bytes 1560
  2.0 58.8 %shard_map.41 = (f32[384,1536]{1,0:T(8,128)S(1)}, f32[384,1536]{1,0:T(8,128)S(1)}) custom-call(bf16[48,256]{1,0:T(8,128)(2,1)S(1)} %bitcast.1, f32[384]{0:T(512)S(1)} %copy-done.1), custom_call_target="tpu_custom_call" | custom-call | tf_op jit(solution)/shard_map/pallas_call | solution.py:275
  60.9 1.4 %copy.6 = f32[384,1536]{1,0:T(8,128)} copy(f32[384,1536]{1,0:T(8,128)S(1)} %get-tuple-element.2) | data formatting | bytes 4718592
  62.3 1.4 %copy.7 = f32[384,1536]{1,0:T(8,128)} copy(f32[384,1536]{1,0:T(8,128)S(1)} %get-tuple-element.3) | data formatting | bytes 4718592
Async XLA Ops:
  0.6 0.7 %copy-start = (bf16[1,1,48,256]{3,2,1,0:T(8,128)(2,1)S(1)}, bf16[1,1,48,256]{3,2,1,0:T(8,128)(2,1)}, u32[]{:S(2)}) copy-start(bf16[1,1,48,256]{3,2,1,0:T(8,128)(2,1)} %param.2) | copy-start | bytes 73732
  1.4 0.7 %copy-start.1 = (f32[384]{0:T(512)S(1)}, f32[384]{0:T(512)}, u32[]{:S(2)}) copy-start(f32[384]{0:T(512)} %prefr_ref.1) | copy-start | bytes 4612
